TPU v7x, 32 devices: a whole 2x2x4 slice. The times are simulated.
32 devices in a mesh: wide: 8 (over y, x, core), narrow: 4 (over z).
Axes of the slice: x: 2, y: 2, z: 4, core: 2. Of those that a mesh axis runs over, the one named last changes fastest.
Arguments:
- features: bfloat16 [131072, 512], P(('wide', 'narrow')), may hold values from -6 to 6
- adjacency: bfloat16 [3072, 128, 128], P(('wide', 'narrow')), may hold values from -0.375 to 0.375
- block_rows: int32 [32, 96], P(('wide', 'narrow')), may hold values from 0 to 31, as said below
- block_cols: int32 [32, 96], P(('wide', 'narrow')), may hold values from 0 to 39, as said below
- block_count: int32 [32], P(('wide', 'narrow')), may hold values from 40 to 96, as said below
- node_count: int32 [32], P(('wide', 'narrow')), may hold values from 2048 to 4096, as said below
- halo_index: int32 [32, 4, 256], P(('wide', 'narrow')), may hold values from 0 to 2047, as said below
- weight: bfloat16 [512, 512], replicated, may hold values from -0.25 to 0.25
- bias: float32 [512], replicated, may hold values from -3 to 3
- out_grad: bfloat16 [131072, 512], P(('wide', 'narrow')), may hold values from -6 to 6
Outputs:
- output: bfloat16 [131072, 512], P(('wide', 'narrow'))
- input_grad: bfloat16 [131072, 512], P(('wide', 'narrow'))
- weight_grad: float32 [512, 512], replicated
- bias_grad: float32 [512], replicated
Inputs may be any that keep to these rules, and one draw needn't show every extreme that they name: `block_count`: each device's live slots include every one of its 32 diagonal blocks and every one of its 8 halo column blocks at least once; some device has all 96 slots live. `block_rows`: within range for live and non-live slots. `block_cols`: within range for live and non-live slots. `node_count`: some device has all 4096 slots live. `halo_index`: the 1024 rows of one device are distinct and all live.
All inputs are finite; a program needn't handle non-finite values.
Results may differ from a plain program's by a relative error of at most 0.0062.
Values may be sent and summed in bfloat16 or wider, within the bound.
A program may use at most 192 MiB of HBM per device.

v0:
```python
import math

import jax
import jax.numpy as jnp
from jax import lax
from jax.sharding import PartitionSpec as P


def with_halo(cells, sides, width):
    for axis, dim in sides:
        count = lax.axis_size(axis)
        ends = count - 1
        head = lax.slice_in_dim(cells, 0, width, axis=dim)
        tail = lax.slice_in_dim(cells, cells.shape[dim] - width, cells.shape[dim], axis=dim)
        cells = jnp.concatenate(
            [
                lax.ppermute(tail, axis, [(i, (i + 1) % count) for i in range(ends)]),
                cells,
                lax.ppermute(head, axis, [((i + 1) % count, i) for i in range(ends)]),
            ],
            axis=dim,
        )
    return cells


def local(
    features,
    adjacency,
    block_rows,
    block_cols,
    block_count,
    node_count,
    halo_index,
    weight,
    bias,
    out_grad,
):
    nodes, width = features.shape
    side = adjacency.shape[1]
    row_blocks = nodes // side
    slots = adjacency.shape[0]
    rows = block_rows[0]
    cols = block_cols[0]
    live = jnp.arange(slots) < block_count[0]
    keep = (jnp.arange(nodes) < node_count[0])[:, None]
    masked = jnp.where(keep, features, jnp.zeros_like(features))
    picks = halo_index[0]
    packed = masked[picks]
    got_wide = with_halo(packed[0:2], (("wide", 0),), 1)
    got_narrow = with_halo(packed[2:4], (("narrow", 0),), 1)
    extended = jnp.concatenate([masked, got_wide[0], got_wide[3], got_narrow[0], got_narrow[3]], 0)
    col_blocks = extended.shape[0] // side
    tiles = extended.reshape(col_blocks, side, width)[cols]
    terms = jnp.einsum("bij,bjf->bif", adjacency, tiles, preferred_element_type=jnp.float32)
    row_target = jnp.where(live, rows, row_blocks)
    summed = (
        jnp.zeros((row_blocks + 1, side, width), jnp.float32).at[row_target].add(terms)[:row_blocks]
    )
    aggregated = summed.reshape(nodes, width).astype(jnp.bfloat16)
    pre = jnp.dot(aggregated, weight, preferred_element_type=jnp.float32) + bias
    sig = jax.nn.sigmoid(pre)
    output = jnp.where(keep, pre * sig, jnp.float32(0.0)).astype(jnp.bfloat16)
    dpre = jnp.where(
        keep, out_grad.astype(jnp.float32) * sig * (1.0 + pre * (1.0 - sig)), jnp.float32(0.0)
    ).astype(jnp.bfloat16)
    weight_part = jnp.dot(aggregated.T, dpre, preferred_element_type=jnp.float32)
    bias_part = jnp.sum(dpre.astype(jnp.float32), 0)
    weight_mid, bias_mid = lax.psum((weight_part, bias_part), "narrow")
    weight_total, bias_total = lax.psum((weight_mid, bias_mid), "wide")
    scale = 1.0 / math.sqrt(nodes * lax.axis_size("wide") * lax.axis_size("narrow"))
    back = jnp.dot(dpre, weight.T, preferred_element_type=jnp.float32).astype(jnp.bfloat16)
    back_tiles = back.reshape(row_blocks, side, width)[rows]
    back_terms = jnp.einsum(
        "bji,bjf->bif", adjacency, back_tiles, preferred_element_type=jnp.float32
    )
    col_target = jnp.where(live, cols, col_blocks)
    spread = (
        jnp.zeros((col_blocks + 1, side, width), jnp.float32)
        .at[col_target]
        .add(back_terms)[:col_blocks]
    )
    own_part = spread[:row_blocks].reshape(nodes, width)
    halo_part = spread[row_blocks:].reshape(4, picks.shape[1], width).astype(jnp.bfloat16)
    ret_wide = with_halo(halo_part[0:2], (("wide", 0),), 1)
    ret_narrow = with_halo(halo_part[2:4], (("narrow", 0),), 1)
    incoming = jnp.concatenate([ret_wide[0], ret_wide[3], ret_narrow[0], ret_narrow[3]], 0).astype(
        jnp.float32
    )
    total_grad = own_part.at[picks.reshape(-1)].add(incoming)
    input_grad = jnp.where(keep, total_grad, jnp.float32(0.0)).astype(jnp.bfloat16)
    return (output, input_grad, weight_total * scale, bias_total * scale)


def solution(mesh):
    placed = (
        P(("wide", "narrow"), None),
        P(("wide", "narrow"), None, None),
        P(("wide", "narrow"), None),
        P(("wide", "narrow"), None),
        P(("wide", "narrow")),
        P(("wide", "narrow")),
        P(("wide", "narrow"), None, None),
        P(),
        P(),
        P(("wide", "narrow"), None),
    )
    return jax.shard_map(
        local,
        mesh=mesh,
        in_specs=placed,
        out_specs=(P(("wide", "narrow"), None), P(("wide", "narrow"), None), P(), P()),
        check_vma=False,
    )
```

profile of v0, /device:TPU:0, one launch (start us, length us, event | category | flops | bytes accessed | tf_op | source)
XLA Modules:
  0.0 405.6 jit_solution(4468749429494696545)
XLA Ops:
  7.2 0.0 all-reduce.3.cloned.1.call-start
  8.0 0.8 fusion.9
  8.8 5.4 %constant_dynamic-update-slice_fusion = (bf16[5120,512]{1,0:T(8,128)(2,1)}, bf16[4096,512]{1,0:T(8,128)(2,1)}) fusion(bf16[4096,512]{1,0:T(8,128)(2,1)} %param.10, pred[4096]{0:T(1024)(128)(4,1)S(1)} %iota_compare_fusion), kind=kLoop, calls=%fused_computation.37 | loop fusion | flops 2097151 | bytes 12587008
  14.2 7.9 %gather_fusion = bf16[1024,512]{1,0:T(8,128)(2,1)} fusion(bf16[4096,512]{1,0:T(8,128)(2,1)} %get-tuple-element.7, s32[1024]{0:T(1024)S(1)} %broadcast_clamp_fusion), kind=kCustom, calls=%fused_computation | custom fusion | bytes 2101248 | tf_op jit(solution)/shard_map/gather | solution.py:48
  22.1 1.3 slice_bitcast_fusion
  23.4 2.4 collective-permute-start
  25.8 1.3 collective-permute-start.1
  27.1 4.3 %collective-permute-start.2 = (bf16[1,256,512]{2,1,0:T(8,128)(2,1)S(1)}, bf16[1,256,512]{2,1,0:T(8,128)(2,1)S(1)}, u32[]{:S(2)}, u32[]{:S(2)}) collective-permute-start(bf16[1,256,512]{2,1,0:T(8,128)(2,1)S(1)} %get-tuple-element.14), channel_id=1, source_target_pairs={{0,1},{1,2},{2,3},{4,5},{5,6},{6,7},{8,9},{9,10},{10,11},{12,13},{... | collective-permute-start | bytes 786440 | tf_op jit(solution)/shard_map/ppermute | solution.py:17
  31.4 1.3 collective-permute-start.3
  33.4 0.6 copy.23
  34.0 0.7 bitcast_dynamic-update-slice_fusion.3
  34.7 0.7 bitcast_dynamic-update-slice_fusion.2
  35.4 1.2 collective-permute-done.2
  36.6 0.7 bitcast_dynamic-update-slice_fusion.1
  37.4 4.0 collective-permute-done.3
  41.3 0.7 bitcast_dynamic-update-slice_fusion
  42.0 9.4 %gather_fusion.1 = bf16[96,128,512]{2,1,0:T(8,128)(2,1)} fusion(bf16[40,128,512]{2,1,0:T(8,128)(2,1)} %bitcast.70, s32[1024]{0:T(1024)S(1)} %pad_clamp_fusion.1), kind=kCustom, calls=%fused_computation.1 | custom fusion | bytes 25166208 | tf_op jit(solution)/shard_map/gather | solution.py:53
  51.4 12.8 %convolution_bitcast_fusion.1 = f32[96,128,512]{1,2,0:T(8,128)} fusion(bf16[96,128,512]{2,1,0:T(8,128)(2,1)} %gather_fusion.1, bf16[96,128,128]{2,1,0:T(8,128)(2,1)S(1)} %copy-done), kind=kOutput, calls=%fused_computation.7 | convolution fusion | flops 1610612736 | bytes 40894464 | tf_op jit(solution)/shard_map/bij,bjf->bif/dot_general | solution.py:54
  64.2 24.7 %copy.17 = f32[96,128,512]{2,1,0:T(8,128)} copy(f32[96,128,512]{1,2,0:T(8,128)} %convolution_bitcast_fusion.1) | data formatting | bytes 50331648 | tf_op jit(solution)/shard_map/bij,bjf->bif/dot_general | solution.py:54
  88.9 4.4 %broadcast_in_dim.49 = f32[33,128,512]{2,1,0:T(8,128)} broadcast(f32[]{:T(128)} %constant.10.clone.1), dimensions={} | broadcast | bytes 8650756 | tf_op jit(solution)/shard_map/broadcast_in_dim | solution.py:57
  93.3 54.2 %scatter_fusion = f32[33,128,512]{2,1,0:T(8,128)} fusion(f32[33,128,512]{2,1,0:T(8,128)} %broadcast_in_dim.49, s32[96]{0:T(128)S(1)} %get-tuple-element.21, f32[96,128,512]{2,1,0:T(8,128)} %copy.17), kind=kCustom, calls=%fused_computation.3 | custom fusion | flops 6291456 | bytes 75497856 | tf_op jit(solution)/shard_map/scatter-add | solution.py:57
  147.5 4.2 %slice.103 = bf16[32,128,512]{2,1,0:T(8,128)(2,1)S(1)} slice(f32[33,128,512]{2,1,0:T(8,128)} %scatter_fusion), slice={[0:32], [0:128], [0:512]} | slice | bytes 8388608 | tf_op jit(solution)/shard_map/slice | solution.py:57
  151.7 0.4 copy-done.5
  152.1 0.1 copy-done.6
  152.2 7.9 %convert_reduce_fusion = (f32[512]{0:T(512)S(1)}, bf16[4096,512]{1,0:T(8,128)(2,1)S(1)}, bf16[4096,512]{1,0:T(8,128)(2,1)}) fusion(f32[512]{0:T(512)S(1)} %copy-done.7, bf16[4096,512]{1,0:T(8,128)(2,1)S(1)} %copy-done.5, pred[4096]{0:T(1024)(128)(4,1)S(1)} %iota_compare_fusion, bf16[4096,512]{1,0:T(8,128)(2,1)S(1)} %bitcast.73, ...), kind=kOutput, calls=%fused_computation.9 | convolution fusion | flops 2183134720 | bytes 17309696 | tf_op jit(solution)/shard_map/dot_general | solution.py:60
  160.1 4.4 %convolution_convert_fusion = bf16[4096,512]{1,0:T(8,128)(2,1)} fusion(bf16[4096,512]{1,0:T(8,128)(2,1)S(1)} %get-tuple-element.5, bf16[512,512]{1,0:T(8,128)(2,1)S(1)} %copy-done.6), kind=kOutput, calls=%fused_computation.14 | convolution fusion | flops 2149580800 | bytes 8912896 | tf_op jit(solution)/shard_map/dot_general | solution.py:71
  164.4 3.3 fusion.15
  167.8 0.2 all-reduce.5.cloned.1.call-start
  168.0 9.1 %gather_fusion.2 = bf16[96,128,512]{2,1,0:T(8,128)(2,1)} fusion(bf16[32,128,512]{2,1,0:T(8,128)(2,1)} %bitcast.71, s32[1024]{0:T(1024)S(1)} %pad_clamp_fusion), kind=kCustom, calls=%fused_computation.2 | custom fusion | bytes 25166208 | tf_op jit(solution)/shard_map/gather | solution.py:72
  177.1 13.0 %convolution_bitcast_fusion = f32[96,128,512]{1,2,0:T(8,128)} fusion(bf16[96,128,512]{2,1,0:T(8,128)(2,1)} %gather_fusion.2, bf16[96,128,128]{2,1,0:T(8,128)(2,1)S(1)} %copy-done), kind=kOutput, calls=%fused_computation.6 | convolution fusion | flops 1610612736 | bytes 40894464 | tf_op jit(solution)/shard_map/bji,bjf->bif/dot_general | solution.py:73
  190.1 24.8 %copy.19 = f32[96,128,512]{2,1,0:T(8,128)} copy(f32[96,128,512]{1,2,0:T(8,128)} %convolution_bitcast_fusion) | data formatting | bytes 50331648 | tf_op jit(solution)/shard_map/bji,bjf->bif/dot_general | solution.py:73
  214.8 5.4 %broadcast_in_dim.53 = f32[41,128,512]{2,1,0:T(8,128)} broadcast(f32[]{:T(128)} %constant.10.clone.1), dimensions={} | broadcast | bytes 10747908 | tf_op jit(solution)/shard_map/broadcast_in_dim | solution.py:78
  220.2 55.3 %scatter_fusion.1 = f32[41,128,512]{2,1,0:T(8,128)} fusion(f32[41,128,512]{2,1,0:T(8,128)} %broadcast_in_dim.53, s32[96]{0:T(128)S(1)} %get-tuple-element.19, f32[96,128,512]{2,1,0:T(8,128)} %copy.19), kind=kCustom, calls=%fused_computation.4 | custom fusion | flops 6291456 | bytes 75497856 | tf_op jit(solution)/shard_map/scatter-add | solution.py:80
  275.5 4.9 %convert.7 = bf16[41,128,512]{2,1,0:T(8,128)(2,1)S(1)} convert(f32[41,128,512]{2,1,0:T(8,128)} %scatter_fusion.1) | non-fusion elementwise | flops 2686976 | bytes 16121856 | tf_op jit(solution)/shard_map/convert
  280.4 1.0 fusion.14
  281.4 2.5 collective-permute-start.4
  283.9 1.3 collective-permute-start.5
  285.2 4.8 %collective-permute-start.6 = (bf16[1,256,512]{2,1,0:T(8,128)(2,1)}, bf16[1,256,512]{2,1,0:T(8,128)(2,1)}, u32[]{:S(2)}, u32[]{:S(2)}) collective-permute-start(bf16[1,256,512]{2,1,0:T(8,128)(2,1)} %bitcast.28), channel_id=1, source_target_pairs={{0,1},{1,2},{2,3},{4,5},{5,6},{6,7},{8,9},{9,10},{10,11},{12,13},{... | collective-permute-start | bytes 786440 | tf_op jit(solution)/shard_map/ppermute | solution.py:17
  290.0 1.3 collective-permute-start.7
  291.3 8.2 %slice.93 = f32[32,128,512]{2,1,0:T(8,128)} slice(f32[41,128,512]{2,1,0:T(8,128)} %scatter_fusion.1), slice={[0:32], [0:128], [0:512]} | slice | bytes 16777216 | tf_op jit(solution)/shard_map/slice | solution.py:82
  299.5 11.2 %psum.30 = f32[512]{0:T(512)S(1)} all-reduce(f32[512]{0:T(512)S(1)} %get-tuple-element.4), channel_id=1, replica_groups=mesh['wide'=8,'narrow'=4] {'narrow'}, use_global_device_ids=true, to_apply=%region_6.7 | all-reduce | flops 512 | bytes 4096 | tf_op jit(solution)/shard_map/psum | solution.py:68
  310.8 13.9 %psum.31 = f32[512]{0:T(512)S(1)} all-reduce(f32[512]{0:T(512)S(1)} %psum.30), channel_id=1, replica_groups=mesh['wide'=8,'narrow'=4] {'wide'}, use_global_device_ids=true, to_apply=%region_7.8 | all-reduce | flops 512 | bytes 4096 | tf_op jit(solution)/shard_map/psum | solution.py:69
  324.6 0.6 broadcast_multiply_fusion.1
  325.2 14.2 %scatter_custom_fusion.2 = f32[4096,512]{1,0:T(8,128)} fusion(f32[4096,512]{1,0:T(8,128)} %bitcast.72, s32[1024]{0:T(1024)S(1)} %bitcast.79, bf16[256,512]{1,0:T(8,128)(2,1)} %bitcast.31, bf16[]{:T(256)} %constant.7, bf16[256,512]{1,0:T(8,128)(2,1)} %bitcast.29, bf16[256,512]{1,0:T(8,128)(2,1)} %bitcast.27, bf16[256,512]{1,0:T(8,128)(2,1)S(1)} %bitcast.75), kind=kCustom, calls=%fused_computation.16 | custom fusion | flops 4718592 | bytes 9437696 | tf_op jit(solution)/shard_map/scatter-add | solution.py:89
  339.5 0.0 all-reduce.5.cloned.1.call-update
  339.5 5.1 %select_convert_fusion = bf16[4096,512]{1,0:T(8,128)(2,1)} fusion(f32[4096,512]{1,0:T(8,128)} %scatter_custom_fusion.2, pred[4096]{0:T(1024)(128)(4,1)S(1)} %iota_compare_fusion), kind=kLoop, calls=%fused_computation.10 | loop fusion | flops 2097152 | bytes 12587008 | tf_op jit(solution)/shard_map/convert_element_type | solution.py:90
  344.6 51.8 %all-reduce.5.cloned.1.call-done = f32[512,512]{1,0:T(8,128)} async-done(((f32[512,512]{1,0:T(8,128)}), f32[512,512]{1,0:T(8,128)}) %all-reduce.5.cloned.1.call-update) | async-done | bytes 1048592 | tf_op jit(solution)/shard_map/psum | solution.py:69
  396.5 2.3 broadcast_multiply_fusion
  (29 shorter events, 0.1 us)
Async XLA Ops:
  7.2 44.2 %copy-start = (bf16[96,128,128]{2,1,0:T(8,128)(2,1)S(1)}, bf16[96,128,128]{2,1,0:T(8,128)(2,1)}, u32[]{:S(2)}) copy-start(bf16[96,128,128]{2,1,0:T(8,128)(2,1)} %param.11) | copy-start | bytes 9437188
  7.2 332.3 %all-reduce.3.cloned.1.call-start = ((), (), s32[]{:S(2)}) async-start(), calls=%async_computation | async-start | bytes 2097152 | tf_op jit(solution)/shard_map/psum | solution.py:68
  14.2 19.1 %copy-start.3 = (s32[1,96]{1,0:T(1,128)S(1)}, s32[1,96]{1,0:T(1,128)}, u32[]{:S(2)}) copy-start(s32[1,96]{1,0:T(1,128)} %param.13) | copy-start | bytes 1156
  14.2 19.1 %copy-start.4 = (s32[1,96]{1,0:T(1,128)S(1)}, s32[1,96]{1,0:T(1,128)}, u32[]{:S(2)}) copy-start(s32[1,96]{1,0:T(1,128)} %param.12) | copy-start | bytes 1156
  14.2 19.2 %copy-start.1 = (s32[1,4,256]{2,1,0:T(4,128)S(1)}, s32[1,4,256]{2,1,0:T(4,128)}, u32[]{:S(2)}) copy-start(s32[1,4,256]{2,1,0:T(4,128)} %param.16) | copy-start | bytes 12292
  23.4 10.7 %collective-permute-start = (bf16[1,256,512]{2,1,0:T(8,128)(2,1)S(1)}, bf16[1,256,512]{2,1,0:T(8,128)(2,1)S(1)}, u32[]{:S(2)}, u32[]{:S(2)}) collective-permute-start(bf16[1,256,512]{2,1,0:T(8,128)(2,1)S(1)} %get-tuple-element.16), channel_id=1, source_target_pairs={{0,4},{4,8},{8,12},{12,16},{16,20},{20,24},{24,28},{1,5},{5,9},{9,... | collective-permute-start | bytes 786440 | tf_op jit(solution)/shard_map/ppermute | solution.py:17
  25.8 9.0 %collective-permute-start.1 = (bf16[1,256,512]{2,1,0:T(8,128)(2,1)S(1)}, bf16[1,256,512]{2,1,0:T(8,128)(2,1)S(1)}, u32[]{:S(2)}, u32[]{:S(2)}) collective-permute-start(bf16[1,256,512]{2,1,0:T(8,128)(2,1)S(1)} %get-tuple-element.15), channel_id=1, source_target_pairs={{4,0},{8,4},{12,8},{16,12},{20,16},{24,20},{28,24},{5,1},{9,5},{13... | collective-permute-start | bytes 786440 | tf_op jit(solution)/shard_map/ppermute | solution.py:19
  27.1 9.6 %collective-permute-start.2 = (bf16[1,256,512]{2,1,0:T(8,128)(2,1)S(1)}, bf16[1,256,512]{2,1,0:T(8,128)(2,1)S(1)}, u32[]{:S(2)}, u32[]{:S(2)}) collective-permute-start(bf16[1,256,512]{2,1,0:T(8,128)(2,1)S(1)} %get-tuple-element.14), channel_id=1, source_target_pairs={{0,1},{1,2},{2,3},{4,5},{5,6},{6,7},{8,9},{9,10},{10,11},{12,13},{... | collective-permute-start | bytes 786440 | tf_op jit(solution)/shard_map/ppermute | solution.py:17
  31.4 9.9 %collective-permute-start.3 = (bf16[1,256,512]{2,1,0:T(8,128)(2,1)S(1)}, bf16[1,256,512]{2,1,0:T(8,128)(2,1)S(1)}, u32[]{:S(2)}, u32[]{:S(2)}) collective-permute-start(bf16[1,256,512]{2,1,0:T(8,128)(2,1)S(1)} %get-tuple-element.13), channel_id=1, source_target_pairs={{1,0},{2,1},{3,2},{5,4},{6,5},{7,6},{9,8},{10,9},{11,10},{13,12},{... | collective-permute-start | bytes 786440 | tf_op jit(solution)/shard_map/ppermute | solution.py:19
  147.5 4.6 %copy-start.5 = (bf16[4096,512]{1,0:T(8,128)(2,1)S(1)}, bf16[4096,512]{1,0:T(8,128)(2,1)}, u32[]{:S(2)}) copy-start(bf16[4096,512]{1,0:T(8,128)(2,1)} %param.19) | copy-start | bytes 12582916
  147.5 4.7 %copy-start.6 = (bf16[512,512]{1,0:T(8,128)(2,1)S(1)}, bf16[512,512]{1,0:T(8,128)(2,1)}, u32[]{:S(2)}) copy-start(bf16[512,512]{1,0:T(8,128)(2,1)} %param.17) | copy-start | bytes 1572868
  147.5 4.7 %copy-start.7 = (f32[512]{0:T(512)S(1)}, f32[512]{0:T(512)}, u32[]{:S(2)}) copy-start(f32[512]{0:T(512)} %param.18) | copy-start | bytes 6148
  167.8 228.7 %all-reduce.5.cloned.1.call-start = ((), (), s32[]{:S(2)}) async-start(), calls=%async_computation.1 | async-start | bytes 2097152 | tf_op jit(solution)/shard_map/psum | solution.py:69
  275.5 15.8 %copy-start.2 = (s32[1,1,4,256]{3,1,2,0:T(1,128)S(1)}, s32[1,1,4,256]{3,1,2,0:T(1,128)}, u32[]{:S(2)}) copy-start(s32[1,1,4,256]{3,1,2,0:T(1,128)} %copy.23) | copy-start | bytes 12292
  281.4 43.8 %collective-permute-start.4 = (bf16[1,256,512]{2,1,0:T(8,128)(2,1)}, bf16[1,256,512]{2,1,0:T(8,128)(2,1)S(1)}, u32[]{:S(2)}, u32[]{:S(2)}) collective-permute-start(bf16[1,256,512]{2,1,0:T(8,128)(2,1)} %bitcast.24), channel_id=1, source_target_pairs={{0,4},{4,8},{8,12},{12,16},{16,20},{20,24},{24,28},{1,5},{5,9},{9,... | collective-permute-start | bytes 786440 | tf_op jit(solution)/shard_map/ppermute | solution.py:17
  283.9 41.3 %collective-permute-start.5 = (bf16[1,256,512]{2,1,0:T(8,128)(2,1)}, bf16[1,256,512]{2,1,0:T(8,128)(2,1)}, u32[]{:S(2)}, u32[]{:S(2)}) collective-permute-start(bf16[1,256,512]{2,1,0:T(8,128)(2,1)} %bitcast.26), channel_id=1, source_target_pairs={{4,0},{8,4},{12,8},{16,12},{20,16},{24,20},{28,24},{5,1},{9,5},{13... | collective-permute-start | bytes 786440 | tf_op jit(solution)/shard_map/ppermute | solution.py:19
  285.2 40.0 %collective-permute-start.6 = (bf16[1,256,512]{2,1,0:T(8,128)(2,1)}, bf16[1,256,512]{2,1,0:T(8,128)(2,1)}, u32[]{:S(2)}, u32[]{:S(2)}) collective-permute-start(bf16[1,256,512]{2,1,0:T(8,128)(2,1)} %bitcast.28), channel_id=1, source_target_pairs={{0,1},{1,2},{2,3},{4,5},{5,6},{6,7},{8,9},{9,10},{10,11},{12,13},{... | collective-permute-start | bytes 786440 | tf_op jit(solution)/shard_map/ppermute | solution.py:17
  290.0 35.2 %collective-permute-start.7 = (bf16[1,256,512]{2,1,0:T(8,128)(2,1)}, bf16[1,256,512]{2,1,0:T(8,128)(2,1)}, u32[]{:S(2)}, u32[]{:S(2)}) collective-permute-start(bf16[1,256,512]{2,1,0:T(8,128)(2,1)} %bitcast.30), channel_id=1, source_target_pairs={{1,0},{2,1},{3,2},{5,4},{6,5},{7,6},{9,8},{10,9},{11,10},{13,12},{... | collective-permute-start | bytes 786440 | tf_op jit(solution)/shard_map/ppermute | solution.py:19
Sparse Core Ops, SparseCore 0:
  167.9 53.9 all-reduce.2
  339.6 56.8 all-reduce.4
where the time goes:
time: 407 us; the launch traced here: 406 us
  other arithmetic  143 us (35%)
  local copies, waits for them, and re-layouts  104 us (26%)
  waiting for transfers between devices  57 us (14%)
  matrix products  41.4 us (10%)
  blocking collectives  25.1 us (6%)
  starting transfers between devices  19.4 us (5%)
  between operations  15.7 us (4%)
    scatter-add x1, other arithmetic, local(): spread = jnp.zeros((col_blocks + 1, side, width), jnp.float32).at[col_tar...  55.3 us
    scatter-add x1, other arithmetic, local(): jnp.zeros((row_blocks + 1, side, width), jnp.float32).at[row_target]  54.2 us
    psum x1, waiting for transfers between devices, local(): weight_total, bias_total = lax.psum((weight_mid, bias_mid), 'wide')  51.8 us
    dot_general x1, local copies, waits for them, and re-layouts, local(): jnp.einsum('bji,bjf->bif', adjacency, back_tiles, preferred_element_type=...  24.8 us
    dot_general x1, local copies, waits for them, and re-layouts, local(): jnp.einsum('bij,bjf->bif', adjacency, tiles, preferred_element_type=jnp.f...  24.7 us
    scatter-add x1, other arithmetic, local(): total_grad = own_part.at[picks.reshape(-1)].add(incoming)  14.2 us
    ppermute x4, starting transfers between devices, with_halo(): lax.ppermute(tail, axis, [(i, (i + 1) % count) for i in range(ends)])  14 us
    psum x1, blocking collectives, local(): weight_total, bias_total = lax.psum((weight_mid, bias_mid), 'wide')  13.9 us
  transfers between devices with their start and end apart: 10, of which 3 were waited for; matrix products, arithmetic and copies ran while one was open for 36% of the time, Pallas kernels for 0%

commit v1 on v0

v1 whole, which is shorter than its diff:
```python
import functools
import math

import jax
import jax.numpy as jnp
from jax import lax
from jax.experimental import pallas as pl
from jax.experimental.pallas import tpu as pltpu
from jax.sharding import PartitionSpec as P

MESH = pl.DeviceIdType.MESH
ANY = pl.ANY
VMEM_LIMIT = 60 * 1024 * 1024


def neighbours(n_wide, n_narrow):
    w = lax.axis_index("wide")
    n = lax.axis_index("narrow")
    return (
        (w > 0, (w - 1, n)),
        (w < n_wide - 1, (w + 1, n)),
        (n > 0, (w, n - 1)),
        (n < n_narrow - 1, (w, n + 1)),
    )


def halo_copy(src, dst, send, recv, k, target):
    return pltpu.make_async_remote_copy(
        src_ref=src.at[k],
        dst_ref=dst.at[k ^ 1],
        send_sem=send.at[k],
        recv_sem=recv.at[k ^ 1],
        device_id=target,
        device_id_type=MESH,
    )


def gather_kernel(n_wide, n_narrow, idx_ref, feat_hbm, halo_ref, feat, packed, load, send, recv):
    count = idx_ref.shape[1]
    span = feat.shape[0]
    fetch = pltpu.make_async_copy(feat_hbm.at[pl.ds(0, span)], feat, load)
    fetch.start()
    near = neighbours(n_wide, n_narrow)
    barrier = pltpu.get_barrier_semaphore()
    for there, target in near:

        @pl.when(there)
        def _():
            pl.semaphore_signal(barrier, inc=1, device_id=target, device_id_type=MESH)

    pl.semaphore_wait(barrier, sum(there.astype(jnp.int32) for there, _ in near))
    fetch.wait()
    lane = lax.broadcasted_iota(jnp.int32, (count, 128), 1).astype(jnp.float32)
    for k in (2, 3, 1, 0):
        there, target = near[k]

        @pl.when(there)
        def _():
            row = idx_ref[pl.ds(k, 1), :].astype(jnp.float32)
            column = jnp.transpose(jnp.broadcast_to(row, (128, count)))
            hot = jnp.concatenate(
                [
                    jnp.where(column == lane + float(at), 1.0, 0.0).astype(jnp.bfloat16)
                    for at in range(0, span, 128)
                ],
                axis=1,
            )
            packed[k] = jnp.dot(hot, feat[...], preferred_element_type=jnp.float32).astype(
                jnp.bfloat16
            )
            halo_copy(packed, halo_ref, send, recv, k, target).start()

        @pl.when(jnp.logical_not(there))
        def _():
            halo_ref[k] = jnp.zeros(halo_ref.shape[1:], halo_ref.dtype)

    for k in range(4):
        there, target = near[k]

        @pl.when(there)
        def _():
            copy = halo_copy(packed, halo_ref, send, recv, k, target)
            copy.wait_send()
            halo_copy(packed, halo_ref, send, recv, k ^ 1, target).wait_recv()


def layer_kernel(
    step,
    rows,
    cols,
    live,
    nodes_live,
    feat_hbm,
    halo_hbm,
    adj_hbm,
    grad_hbm,
    w_ref,
    b_ref,
    out_hbm,
    low_hbm,
    high_hbm,
    ret_hbm,
    wg_ref,
    bg_ref,
    ext,
    adj,
    grad,
    acc,
    back,
    out,
    wsum,
    bsum,
    sem,
    out_sem,
):
    row_blocks, side, width = feat_hbm.shape
    halo_blocks = halo_hbm.shape[0]
    col_blocks = row_blocks + halo_blocks
    low_blocks = low_hbm.shape[0]
    count = live[0]
    keep_to = nodes_live[0]
    loads = [
        pltpu.make_async_copy(feat_hbm, ext.at[pl.ds(0, row_blocks)], sem.at[0]),
        pltpu.make_async_copy(halo_hbm, ext.at[pl.ds(row_blocks, halo_blocks)], sem.at[1]),
        pltpu.make_async_copy(adj_hbm, adj, sem.at[2]),
        pltpu.make_async_copy(grad_hbm, grad, sem.at[3]),
    ]
    for load in loads:
        load.start()

    def clear(i, carry):
        acc[i] = jnp.zeros((side, width), jnp.float32)
        return carry

    lax.fori_loop(0, row_blocks + 1, clear, 0)
    wsum[...] = jnp.zeros_like(wsum)
    bsum[...] = jnp.zeros_like(bsum)
    for load in loads[:3]:
        load.wait()

    def kept(block, blocks=1):
        at = lax.broadcasted_iota(jnp.int32, (blocks * side, width), 0)
        return at < keep_to - block * side

    def mask(i, carry):
        ext[i] = jnp.where(kept(i), ext[i].astype(jnp.float32), 0.0).astype(ext.dtype)
        return carry

    lax.fori_loop(keep_to // side, row_blocks, mask, 0)

    unroll = 4
    trips = (count + unroll - 1) // unroll

    def forward(t, carry):
        for u in range(unroll):
            b = t * unroll + u
            to = jnp.where(b < count, rows[b], row_blocks)
            acc[to] += jnp.dot(adj[b], ext[cols[b]], preferred_element_type=jnp.float32)
        return carry

    lax.fori_loop(0, trips, forward, 0)
    loads[3].wait()

    def put(i):
        return pltpu.make_async_copy(
            out.at[pl.ds(i * step, step)], out_hbm.at[pl.ds(i * step, step)], out_sem.at[i]
        )

    tall = step * side

    def dense(i, carry):
        at = pl.ds(i * step, step)
        agg = acc[at].reshape(tall, width).astype(jnp.bfloat16)
        pre = jnp.dot(agg, w_ref[...], preferred_element_type=jnp.float32) + b_ref[...]
        keep = kept(i * step, step)
        sig = jax.nn.sigmoid(pre)
        res = jnp.where(keep, pre * sig, 0.0).astype(jnp.bfloat16)
        out[at] = res.reshape(step, side, width)
        put(i).start()
        g = grad[at].reshape(tall, width).astype(jnp.float32)
        dpre = jnp.where(keep, g * sig * (1.0 + pre * (1.0 - sig)), 0.0).astype(jnp.bfloat16)
        wsum[...] += lax.dot_general(
            agg, dpre, (((0,), (0,)), ((), ())), preferred_element_type=jnp.float32
        )
        bsum[...] += jnp.sum(dpre.astype(jnp.float32).reshape(tall // 8, 8, width), 0)
        back[at] = (
            lax.dot_general(
                dpre, w_ref[...], (((1,), (1,)), ((), ())), preferred_element_type=jnp.float32
            )
            .astype(jnp.bfloat16)
            .reshape(step, side, width)
        )
        return carry

    lax.fori_loop(0, row_blocks // step, dense, 0)
    wg_ref[...] = wsum[...].astype(wg_ref.dtype)
    bg_ref[...] = jnp.sum(bsum[...], 0, keepdims=True)

    lax.fori_loop(0, col_blocks + 1, clear, 0)

    def backward(t, carry):
        for u in range(unroll):
            b = t * unroll + u
            to = jnp.where(b < count, cols[b], col_blocks)
            acc[to] += lax.dot_general(
                adj[b], back[rows[b]], (((0,), (0,)), ((), ())), preferred_element_type=jnp.float32
            )
        return carry

    lax.fori_loop(0, trips, backward, 0)
    low = pltpu.make_async_copy(acc.at[pl.ds(0, low_blocks)], low_hbm, sem.at[0])
    low.start()

    def narrow_halo(i, carry):
        ext[i] = acc[row_blocks + i].astype(ext.dtype)
        return carry

    lax.fori_loop(0, halo_blocks, narrow_halo, 0)
    ret = pltpu.make_async_copy(ext.at[pl.ds(0, halo_blocks)], ret_hbm, sem.at[1])
    ret.start()

    def narrow_high(i, carry):
        grad[i] = jnp.where(kept(i), acc[i], 0.0).astype(grad.dtype)
        return carry

    lax.fori_loop(low_blocks, row_blocks, narrow_high, 0)
    high = pltpu.make_async_copy(
        grad.at[pl.ds(low_blocks, row_blocks - low_blocks)], high_hbm, sem.at[2]
    )
    high.start()
    low.wait()
    ret.wait()
    high.wait()

    def drain(i, carry):
        put(i).wait()
        return carry

    lax.fori_loop(0, row_blocks // step, drain, 0)


def sum_kernel(
    n_wide,
    n_narrow,
    scale,
    idx_ref,
    keep_ref,
    ret_ref,
    wg_ref,
    bg_ref,
    low_hbm,
    grad_ref,
    wout_ref,
    bout_ref,
    low,
    incoming,
    rs_wide,
    rs_narrow,
    part,
    ag_narrow,
    ag_wide,
    b_wide,
    b_mid,
    b_narrow,
    load,
    send,
    recv,
    send_w,
    recv_w,
    send_n,
    recv_n,
    send_gn,
    recv_gn,
    send_gw,
    recv_gw,
    send_bw,
    recv_bw,
    send_bn,
    recv_bn,
):
    w = lax.axis_index("wide")
    n = lax.axis_index("narrow")
    slab = wg_ref.shape[1]
    part_width = rs_narrow.shape[2]
    fetch = pltpu.make_async_copy(low_hbm, low, load)
    fetch.start()

    def wide_peer(d):
        return (lax.rem(w + d, n_wide), n)

    def narrow_peer(d):
        return (w, lax.rem(n + d, n_narrow))

    peers = [wide_peer(d) for d in range(1, n_wide)] + [
        narrow_peer(d) for d in range(1, n_narrow)
    ]
    barrier = pltpu.get_barrier_semaphore()
    for peer in peers:
        pl.semaphore_signal(barrier, inc=1, device_id=peer, device_id_type=MESH)
    pl.semaphore_wait(barrier, len(peers))

    def remote(src, dst, s, r, peer):
        return pltpu.make_async_remote_copy(
            src_ref=src, dst_ref=dst, send_sem=s, recv_sem=r, device_id=peer, device_id_type=MESH
        )

    pending = []
    near = neighbours(n_wide, n_narrow)

    first = []
    for d in range(1, n_wide):
        peer = wide_peer(d)
        c = remote(wg_ref.at[peer[0]], rs_wide.at[d], send_w.at[d], recv_w.at[d], peer)
        c.start()
        first.append(c)
    bias_first = []
    for d in range(1, n_wide):
        c = remote(bg_ref, b_wide.at[d], send_bw.at[d], recv_bw.at[d], wide_peer(d))
        c.start()
        bias_first.append(c)
    for k in (2, 3, 1, 0):
        there, target = near[k]

        @pl.when(there)
        def _():
            halo_copy(ret_ref, incoming, send, recv, k, target).start()

        @pl.when(jnp.logical_not(there))
        def _():
            incoming[k] = jnp.zeros(incoming.shape[1:], incoming.dtype)

    total = wg_ref[w].astype(jnp.float32)
    for c in first:
        c.wait_recv()
    for d in range(1, n_wide):
        total = total + rs_wide[d].astype(jnp.float32)
    bias = bg_ref[...]
    for c in bias_first:
        c.wait_recv()
    for d in range(1, n_wide):
        bias = bias + b_wide[d]
    b_mid[...] = bias
    for j in range(n_narrow):
        part[j] = total[:, j * part_width : (j + 1) * part_width].astype(part.dtype)
    second = []
    for d in range(1, n_narrow):
        peer = narrow_peer(d)
        c = remote(part.at[peer[1]], rs_narrow.at[d], send_n.at[d], recv_n.at[d], peer)
        c.start()
        second.append(c)
    for d in range(1, n_narrow):
        c = remote(b_mid, b_narrow.at[d], send_bn.at[d], recv_bn.at[d], narrow_peer(d))
        c.start()
        bias_first.append(c)
        second.append(c)
    piece = part[n].astype(jnp.float32)
    for c in second:
        c.wait_recv()
    for d in range(1, n_narrow):
        piece = piece + rs_narrow[d].astype(jnp.float32)
        bias = bias + b_narrow[d]
    bout_ref[...] = bias * scale
    ag_narrow[n] = (piece * scale).astype(ag_narrow.dtype)
    third = []
    for d in range(1, n_narrow):
        c = remote(
            ag_narrow.at[n], ag_narrow.at[n], send_gn.at[d], recv_gn.at[d], narrow_peer(d)
        )
        c.start()
        third.append(c)
    for c in third:
        c.wait_recv()
    fourth = []
    for d in range(1, n_wide):
        c = remote(ag_narrow, ag_wide.at[w], send_gw.at[d], recv_gw.at[d], wide_peer(d))
        c.start()
        fourth.append(c)
    ag_wide[w] = ag_narrow[...]

    for k in range(4):
        there, target = near[k]

        @pl.when(there)
        def _():
            halo_copy(ret_ref, incoming, send, recv, k, target).wait_send()
            halo_copy(ret_ref, incoming, send, recv, k ^ 1, target).wait_recv()

    fetch.wait()
    chunk = low.shape[1]
    merged = incoming[...].reshape(-1, incoming.shape[2])
    idx = idx_ref[...]
    keep_to = keep_ref[...]

    def scatter(i, carry):
        at = lax.broadcasted_iota(jnp.int32, (chunk, idx.shape[1]), 0) + i * chunk
        hot = jnp.where(at == idx, 1.0, 0.0).astype(jnp.bfloat16)
        full = low[i] + jnp.dot(hot, merged, preferred_element_type=jnp.float32)
        row = lax.broadcasted_iota(jnp.int32, full.shape, 0) + i * chunk
        grad_ref[i] = jnp.where(row < keep_to, full, 0.0).astype(grad_ref.dtype)
        return carry

    lax.fori_loop(0, low.shape[0], scatter, 0)
    for c in fourth:
        c.wait_recv()
    for i in range(n_wide):
        for j in range(n_narrow):
            wout_ref[pl.ds(i * slab, slab), pl.ds(j * part_width, part_width)] = ag_wide[
                i, j
            ].astype(jnp.float32)
    for c in first + bias_first + second[: n_narrow - 1] + third + fourth:
        c.wait_send()


def local(
    n_wide,
    n_narrow,
    features,
    adjacency,
    block_rows,
    block_cols,
    block_count,
    node_count,
    halo_index,
    weight,
    bias,
    out_grad,
):
    nodes, width = features.shape
    slots, side, _ = adjacency.shape
    row_blocks = nodes // side
    sides, halo = halo_index.shape[1:]
    halo_blocks = sides * halo // side
    low_blocks = row_blocks // 2
    col_blocks = row_blocks + halo_blocks
    bf, f32 = jnp.bfloat16, jnp.float32
    picks = halo_index[0]
    vm = pl.BlockSpec(memory_space=pltpu.VMEM)
    sm = pl.BlockSpec(memory_space=pltpu.SMEM)
    hb = pl.BlockSpec(memory_space=ANY)
    dma = pltpu.SemaphoreType.DMA

    halos = pl.pallas_call(
        functools.partial(gather_kernel, n_wide, n_narrow),
        name="halo_out",
        out_shape=jax.ShapeDtypeStruct((sides, halo, width), bf),
        in_specs=[vm, hb],
        out_specs=vm,
        scratch_shapes=[
            pltpu.VMEM((nodes // 2, width), bf),
            pltpu.VMEM((sides, halo, width), bf),
            dma,
            dma((sides,)),
            dma((sides,)),
        ],
        compiler_params=pltpu.CompilerParams(
            collective_id=0, has_side_effects=True, vmem_limit_bytes=VMEM_LIMIT
        ),
    )(picks, features)

    step = 2
    blocked = (row_blocks, side, width)
    out, low, high, ret, wg, bg = pl.pallas_call(
        functools.partial(layer_kernel, step),
        name="layer",
        out_shape=(
            jax.ShapeDtypeStruct(blocked, bf),
            jax.ShapeDtypeStruct((low_blocks, side, width), f32),
            jax.ShapeDtypeStruct((row_blocks - low_blocks, side, width), bf),
            jax.ShapeDtypeStruct((halo_blocks, side, width), bf),
            jax.ShapeDtypeStruct((width, width), bf),
            jax.ShapeDtypeStruct((1, width), f32),
        ),
        in_specs=[sm, sm, sm, sm, hb, hb, hb, hb, vm, vm],
        out_specs=(hb, hb, hb, hb, vm, vm),
        scratch_shapes=[
            pltpu.VMEM((col_blocks, side, width), bf),
            pltpu.VMEM((slots, side, side), bf),
            pltpu.VMEM(blocked, bf),
            pltpu.VMEM((col_blocks + 1, side, width), f32),
            pltpu.VMEM(blocked, bf),
            pltpu.VMEM(blocked, bf),
            pltpu.VMEM((width, width), f32),
            pltpu.VMEM((8, width), f32),
            dma((4,)),
            dma((row_blocks // step,)),
        ],
        compiler_params=pltpu.CompilerParams(vmem_limit_bytes=VMEM_LIMIT),
    )(
        block_rows[0],
        block_cols[0],
        block_count,
        node_count,
        features.reshape(blocked),
        halos.reshape(halo_blocks, side, width),
        adjacency,
        out_grad.reshape(blocked),
        weight,
        bias.reshape(1, width),
    )

    slab = width // n_wide
    part_width = width // n_narrow
    scale = 1.0 / math.sqrt(nodes * n_wide * n_narrow)
    chunk = 2 * side
    low_grad, wout, bout = pl.pallas_call(
        functools.partial(sum_kernel, n_wide, n_narrow, scale),
        name="sums",
        out_shape=(
            jax.ShapeDtypeStruct((low_blocks // 2, chunk, width), bf),
            jax.ShapeDtypeStruct((width, width), f32),
            jax.ShapeDtypeStruct((1, width), f32),
        ),
        in_specs=[vm, vm, vm, vm, vm, hb],
        out_specs=(vm, vm, vm),
        scratch_shapes=[
            pltpu.VMEM((low_blocks // 2, chunk, width), f32),
            pltpu.VMEM((sides, halo, width), bf),
            pltpu.VMEM((n_wide, slab, width), bf),
            pltpu.VMEM((n_narrow, slab, part_width), bf),
            pltpu.VMEM((n_narrow, slab, part_width), bf),
            pltpu.VMEM((n_narrow, slab, part_width), bf),
            pltpu.VMEM((n_wide, n_narrow, slab, part_width), bf),
            pltpu.VMEM((n_wide, 1, width), f32),
            pltpu.VMEM((1, width), f32),
            pltpu.VMEM((n_narrow, 1, width), f32),
            dma,
            dma((sides,)),
            dma((sides,)),
        ]
        + [dma((n_wide,))] * 2
        + [dma((n_narrow,))] * 4
        + [dma((n_wide,))] * 4
        + [dma((n_narrow,))] * 2,
        compiler_params=pltpu.CompilerParams(
            collective_id=1, has_side_effects=True, vmem_limit_bytes=VMEM_LIMIT
        ),
    )(
        picks.reshape(1, sides * halo),
        jnp.broadcast_to(node_count.reshape(1, 1), (1, width)),
        ret.reshape(sides, halo, width),
        wg.reshape(n_wide, slab, width),
        bg,
        low.reshape(low_blocks // 2, chunk, width),
    )
    input_grad = jnp.concatenate(
        [low_grad.reshape(-1, width), high.reshape(-1, width)], 0
    )
    return out.reshape(nodes, width), input_grad, wout, bout.reshape(width)


def solution(mesh):
    both = ("wide", "narrow")
    placed = (
        P(both, None),
        P(both, None, None),
        P(both, None),
        P(both, None),
        P(both),
        P(both),
        P(both, None, None),
        P(),
        P(),
        P(both, None),
    )
    return jax.shard_map(
        functools.partial(local, mesh.shape["wide"], mesh.shape["narrow"]),
        mesh=mesh,
        in_specs=placed,
        out_specs=(P(both, None), P(both, None), P(), P()),
        check_vma=False,
    )
```

time: 407 us -> 90.6 us (0.22)
  other arithmetic: 143 us -> 3.96 us
  local copies, waits for them, and re-layouts: 104 us -> 3.43 us
  Pallas kernels: 0 us -> 81.4 us
  waiting for transfers between devices: 57 us -> 0 us
  matrix products: 41.4 us -> 0 us
  blocking collectives: 25.1 us -> 0 us
  starting transfers between devices: 19.4 us -> 0 us
  between operations: 15.7 us -> 1.98 us
    scatter-add x3 -> x0, other arithmetic: 124 us -> none  [the longest x1 55.3 us: local(): spread = jnp.zeros((col_blocks + 1, side, width), jnp.float32).at[col_tar...]
    pallas_call x0 -> x3, Pallas kernels: none -> 81.4 us  [the longest x1 36.2 us: local(): pl.pallas_call(functools.partial(layer_kernel, step), name='layer', out_s...]
    psum x2 -> x0, waiting for transfers between devices: 51.8 us -> none  [the longest x1 51.8 us: local(): weight_total, bias_total = lax.psum((weight_mid, bias_mid), 'wide')]
    dot_general x2 -> x0, local copies, waits for them, and re-layouts: 49.4 us -> none  [the longest x1 24.8 us: local(): jnp.einsum('bji,bjf->bif', adjacency, back_tiles, preferred_element_type=...]
    dot_general x5 -> x0, matrix products: 41.4 us -> none  [the longest x1 13 us: local(): jnp.einsum('bji,bjf->bif', adjacency, back_tiles, preferred_element_type=...]
    gather x3 -> x0, local copies, waits for them, and re-layouts: 26.3 us -> none  [the longest x1 9.35 us: local(): tiles = extended.reshape(col_blocks, side, width)[cols]]
    psum x2 -> x0, blocking collectives: 25.1 us -> none  [the longest x1 13.9 us: local(): weight_total, bias_total = lax.psum((weight_mid, bias_mid), 'wide')]
    ppermute x8 -> x0, starting transfers between devices: 19.2 us -> none  [the longest x4 14 us: with_halo(): lax.ppermute(tail, axis, [(i, (i + 1) % count) for i in range(ends)])]
  transfers between devices with their start and end apart: 10 -> 0, of which waited for: 3 -> 0; matrix products, arithmetic and copies ran while one was open for 36% -> 0% of each run, Pallas kernels for 0% -> 0%
where the time goes in v1:
time: 90.6 us; the launch traced here: 90.7 us
  Pallas kernels  81.4 us (90%)
  other arithmetic  3.96 us (4%)
  local copies, waits for them, and re-layouts  3.43 us (4%)
  between operations  1.98 us (2%)
    pallas_call x1, Pallas kernels, local(): pl.pallas_call(functools.partial(layer_kernel, step), name='layer', out_s...  36.2 us
    pallas_call x1, Pallas kernels, local(): pl.pallas_call(functools.partial(sum_kernel, n_wide, n_narrow, scale), na...  31.5 us
    pallas_call x1, Pallas kernels, local(): pl.pallas_call(functools.partial(gather_kernel, n_wide, n_narrow), name='...  13.6 us
    concatenate x1, other arithmetic, local(): jnp.concatenate([low_grad.reshape(-1, width), high.reshape(-1, width)], 0)  3.96 us
    unnamed x9, local copies, waits for them, and re-layouts  2.84 us

profile of v1, /device:TPU:0, one launch (start us, length us, event | category | flops | bytes accessed | tf_op | source)
XLA Modules:
  0.0 90.7 jit_solution(16527429338890975752)
XLA Ops:
  1.9 0.6 broadcast_in_dim.8.keep_ref
  2.5 1.3 %copy.14 = s32[1,1,4,256]{3,1,2,0:T(1,128)} copy(s32[1,1,4,256]{3,2,1,0:T(4,128)} %bitcast.26) | data formatting | bytes 8192
  3.8 13.6 %halo_out.1 = bf16[4,256,512]{2,1,0:T(8,128)(2,1)} custom-call(s32[4,256]{1,0:T(4,128)} %bitcast.27, bf16[4096,512]{1,0:T(8,128)(2,1)} %feat_hbm.1), custom_call_target="tpu_custom_call" | custom-call | tf_op jit(solution)/shard_map/halo_out/pallas_call | solution.py:442
  17.4 36.2 %layer.1 = (bf16[32,128,512]{2,1,0:T(8,128)(2,1)}, f32[16,128,512]{2,1,0:T(8,128)}, bf16[16,128,512]{2,1,0:T(8,128)(2,1)}, bf16[8,128,512]{2,1,0:T(8,128)(2,1)},...) custom-call(s32[96]{0:T(128)} %bitcast.31, s32[96]{0:T(128)} %bitcast.32, s32[1]{0:T(128)S(6)} %copy.17.live, ...), custom_call_target="tpu_custom_call" | custom-call | tf_op jit(solution)/shard_map/layer/pallas_call | solution.py:462
  53.7 0.0 copy-start
  53.7 31.5 %sums.1 = (bf16[8,256,512]{2,1,0:T(8,128)(2,1)}, f32[512,512]{1,0:T(8,128)}, f32[1,512]{1,0:T(1,128)}) custom-call(s32[1,1024]{1,0:T(1,128)} %bitcast.28, s32[1,512]{1,0:T(1,128)} %broadcast_in_dim.8.keep_ref, bf16[4,256,512]{2,1,0:T(8,128)(2,1)} %bitcast.24, bf16[8,64,512]{2,1,0:T(8,128)(2,1)} %bitcast.25, f32[1,512]{1,0:T(1,128)} %get-tuple-element.16.bg_ref, ...), custom_call_target="tpu_custom_call" | custom-call | tf_op jit(solution)/shard_map/sums/pallas_call | solution.py:505
  85.2 0.0 copy-done
  85.2 0.0 copy-start.1
  85.2 0.0 copy-start.2
  85.2 4.0 %pad_maximum_fusion = bf16[4096,512]{1,0:T(8,128)(2,1)} fusion(bf16[2048,512]{1,0:T(8,128)(2,1)S(1)} %bitcast.22, bf16[2048,512]{1,0:T(8,128)(2,1)} %bitcast.23), kind=kLoop, calls=%fused_computation | loop fusion | flops 8388608 | bytes 8388608 | tf_op jit(solution)/shard_map/concatenate | solution.py:545
  89.2 0.0 copy-done.1
  89.2 1.0 %copy.19 = f32[512,512]{1,0:T(8,128)} copy(f32[512,512]{1,0:T(8,128)S(1)} %copy-done.1) | data formatting | bytes 2097152
  90.1 0.0 copy-done.2
  90.1 0.6 copy.20
Async XLA Ops:
  53.7 31.5 %copy-start = (bf16[16,128,512]{2,1,0:T(8,128)(2,1)S(1)}, bf16[16,128,512]{2,1,0:T(8,128)(2,1)}, u32[]{:S(2)}) copy-start(bf16[16,128,512]{2,1,0:T(8,128)(2,1)} %get-tuple-element.19) | copy-start | bytes 6291460
  85.2 4.0 %copy-start.1 = (f32[512,512]{1,0:T(8,128)S(1)}, f32[512,512]{1,0:T(8,128)}, u32[]{:S(2)}) copy-start(f32[512,512]{1,0:T(8,128)} %get-tuple-element.28) | copy-start | bytes 3145732
  85.2 4.9 %copy-start.2 = (f32[1,512]{1,0:T(1,128)S(1)}, f32[1,512]{1,0:T(1,128)}, u32[]{:S(2)}) copy-start(f32[1,512]{1,0:T(1,128)} %get-tuple-element.21) | copy-start | bytes 6148

commit v2 on v1

--- a/solution.py
+++ b/solution.py
@@ -35,7 +35,51 @@
     )
 
 
-def gather_kernel(n_wide, n_narrow, idx_ref, feat_hbm, halo_ref, feat, packed, load, send, recv):
+def tables(row_ref, col_ref, count, row_blocks, col_blocks):
+    lanes = row_ref.shape[1]
+    f32 = jnp.float32
+    lane = lax.broadcasted_iota(jnp.int32, (lanes, lanes), 1).astype(f32)
+    sub = lax.broadcasted_iota(jnp.int32, (lanes, lanes), 0).astype(f32)
+
+    def spread(x):
+        return jnp.broadcast_to(x.astype(f32), (lanes, lanes))
+
+    halo_blocks = col_blocks - row_blocks
+    col = spread(col_ref[...])
+    place = jnp.where(col >= row_blocks, col - row_blocks, col + halo_blocks)
+    place = jnp.where(lane < spread(count), place, float(col_blocks))
+    place_t = jnp.transpose(place)
+    row_t = jnp.transpose(spread(row_ref[...]))
+    same = place == place_t
+    ahead = lane < sub
+    one = lambda m: jnp.where(m, 1.0, 0.0)
+    rank = jnp.sum(one((place < place_t) | (same & ahead)), 1, keepdims=True)
+    twin = jnp.minimum(jnp.sum(one(same & ahead), 1, keepdims=True), 1.0)
+    hot = one(jnp.broadcast_to(rank, (lanes, lanes)) == lane)
+    pick = lambda x: jnp.sum(hot * x, 0, keepdims=True)
+    ends = jnp.sum(one(place_t <= lane), 0, keepdims=True)
+    keep = pick(jnp.broadcast_to(twin, (lanes, lanes)))
+    return pick(sub), pick(row_t), keep, ends
+
+
+def gather_kernel(
+    n_wide,
+    n_narrow,
+    row_blocks,
+    col_blocks,
+    idx_ref,
+    row_ref,
+    col_ref,
+    count_ref,
+    feat_hbm,
+    halo_ref,
+    table_ref,
+    feat,
+    packed,
+    load,
+    send,
+    recv,
+):
     count = idx_ref.shape[1]
     span = feat.shape[0]
     fetch = pltpu.make_async_copy(feat_hbm.at[pl.ds(0, span)], feat, load)
@@ -48,39 +92,50 @@
         def _():
             pl.semaphore_signal(barrier, inc=1, device_id=target, device_id_type=MESH)
 
-    pl.semaphore_wait(barrier, sum(there.astype(jnp.int32) for there, _ in near))
     fetch.wait()
     lane = lax.broadcasted_iota(jnp.int32, (count, 128), 1).astype(jnp.float32)
+
+    def pack(k):
+        row = idx_ref[pl.ds(k, 1), :].astype(jnp.float32)
+        column = jnp.transpose(jnp.broadcast_to(row, (128, count)))
+        hot = jnp.concatenate(
+            [
+                jnp.where(column == lane + float(at), 1.0, 0.0).astype(jnp.bfloat16)
+                for at in range(0, span, 128)
+            ],
+            axis=1,
+        )
+        packed[k] = jnp.dot(hot, feat[...], preferred_element_type=jnp.float32).astype(
+            jnp.bfloat16
+        )
+
+    pack(2)
+    pl.semaphore_wait(barrier, sum(there.astype(jnp.int32) for there, _ in near))
     for k in (2, 3, 1, 0):
         there, target = near[k]
+        if k != 2:
+            pack(k)
 
         @pl.when(there)
         def _():
-            row = idx_ref[pl.ds(k, 1), :].astype(jnp.float32)
-            column = jnp.transpose(jnp.broadcast_to(row, (128, count)))
-            hot = jnp.concatenate(
-                [
-                    jnp.where(column == lane + float(at), 1.0, 0.0).astype(jnp.bfloat16)
-                    for at in range(0, span, 128)
-                ],
-                axis=1,
-            )
-            packed[k] = jnp.dot(hot, feat[...], preferred_element_type=jnp.float32).astype(
-                jnp.bfloat16
-            )
             halo_copy(packed, halo_ref, send, recv, k, target).start()
 
         @pl.when(jnp.logical_not(there))
         def _():
             halo_ref[k] = jnp.zeros(halo_ref.shape[1:], halo_ref.dtype)
 
+    table_ref[...] = jnp.zeros_like(table_ref)
+    for i, line in enumerate(
+        tables(row_ref, col_ref, count_ref[...], row_blocks, col_blocks)
+    ):
+        table_ref[pl.ds(i, 1), :] = line.astype(jnp.int32)
+
     for k in range(4):
         there, target = near[k]
 
         @pl.when(there)
         def _():
-            copy = halo_copy(packed, halo_ref, send, recv, k, target)
-            copy.wait_send()
+            halo_copy(packed, halo_ref, send, recv, k, target).wait_send()
             halo_copy(packed, halo_ref, send, recv, k ^ 1, target).wait_recv()
 
 
@@ -97,9 +152,7 @@
     w_ref,
     b_ref,
     out_hbm,
-    low_hbm,
-    high_hbm,
-    ret_hbm,
+    back_hbm,
     wg_ref,
     bg_ref,
     ext,
@@ -115,8 +168,6 @@
 ):
     row_blocks, side, width = feat_hbm.shape
     halo_blocks = halo_hbm.shape[0]
-    col_blocks = row_blocks + halo_blocks
-    low_blocks = low_hbm.shape[0]
     count = live[0]
     keep_to = nodes_live[0]
     loads = [
@@ -173,12 +224,12 @@
         agg = acc[at].reshape(tall, width).astype(jnp.bfloat16)
         pre = jnp.dot(agg, w_ref[...], preferred_element_type=jnp.float32) + b_ref[...]
         keep = kept(i * step, step)
-        sig = jax.nn.sigmoid(pre)
-        res = jnp.where(keep, pre * sig, 0.0).astype(jnp.bfloat16)
-        out[at] = res.reshape(step, side, width)
+        sig = 0.5 * jnp.tanh(0.5 * pre) + 0.5
+        act = pre * sig
+        out[at] = jnp.where(keep, act, 0.0).astype(jnp.bfloat16).reshape(step, side, width)
         put(i).start()
         g = grad[at].reshape(tall, width).astype(jnp.float32)
-        dpre = jnp.where(keep, g * sig * (1.0 + pre * (1.0 - sig)), 0.0).astype(jnp.bfloat16)
+        dpre = jnp.where(keep, g * (sig + act * (1.0 - sig)), 0.0).astype(jnp.bfloat16)
         wsum[...] += lax.dot_general(
             agg, dpre, (((0,), (0,)), ((), ())), preferred_element_type=jnp.float32
         )
@@ -196,41 +247,9 @@
     wg_ref[...] = wsum[...].astype(wg_ref.dtype)
     bg_ref[...] = jnp.sum(bsum[...], 0, keepdims=True)
 
-    lax.fori_loop(0, col_blocks + 1, clear, 0)
-
-    def backward(t, carry):
-        for u in range(unroll):
-            b = t * unroll + u
-            to = jnp.where(b < count, cols[b], col_blocks)
-            acc[to] += lax.dot_general(
-                adj[b], back[rows[b]], (((0,), (0,)), ((), ())), preferred_element_type=jnp.float32
-            )
-        return carry
-
-    lax.fori_loop(0, trips, backward, 0)
-    low = pltpu.make_async_copy(acc.at[pl.ds(0, low_blocks)], low_hbm, sem.at[0])
-    low.start()
-
-    def narrow_halo(i, carry):
-        ext[i] = acc[row_blocks + i].astype(ext.dtype)
-        return carry
-
-    lax.fori_loop(0, halo_blocks, narrow_halo, 0)
-    ret = pltpu.make_async_copy(ext.at[pl.ds(0, halo_blocks)], ret_hbm, sem.at[1])
-    ret.start()
-
-    def narrow_high(i, carry):
-        grad[i] = jnp.where(kept(i), acc[i], 0.0).astype(grad.dtype)
-        return carry
-
-    lax.fori_loop(low_blocks, row_blocks, narrow_high, 0)
-    high = pltpu.make_async_copy(
-        grad.at[pl.ds(low_blocks, row_blocks - low_blocks)], high_hbm, sem.at[2]
-    )
-    high.start()
-    low.wait()
-    ret.wait()
-    high.wait()
+    kept_back = pltpu.make_async_copy(back, back_hbm, sem.at[0])
+    kept_back.start()
+    kept_back.wait()
 
     def drain(i, carry):
         put(i).wait()
@@ -239,20 +258,24 @@
     lax.fori_loop(0, row_blocks // step, drain, 0)
 
 
-def sum_kernel(
+def back_kernel(
     n_wide,
     n_narrow,
     scale,
+    table,
+    nodes_live,
     idx_ref,
-    keep_ref,
-    ret_ref,
     wg_ref,
     bg_ref,
-    low_hbm,
+    adj_hbm,
+    back_hbm,
     grad_ref,
     wout_ref,
     bout_ref,
-    low,
+    adj,
+    back,
+    run,
+    ret,
     incoming,
     rs_wide,
     rs_narrow,
@@ -282,8 +305,14 @@
     n = lax.axis_index("narrow")
     slab = wg_ref.shape[1]
     part_width = rs_narrow.shape[2]
-    fetch = pltpu.make_async_copy(low_hbm, low, load)
-    fetch.start()
+    row_blocks, side, width = back.shape
+    slots = adj.shape[0]
+    loads = [
+        pltpu.make_async_copy(back_hbm, back, load.at[0]),
+        pltpu.make_async_copy(adj_hbm, adj, load.at[1]),
+    ]
+    for fetch in loads:
+        fetch.start()
 
     def wide_peer(d):
         return (lax.rem(w + d, n_wide), n)
@@ -318,12 +347,36 @@
         c = remote(bg_ref, b_wide.at[d], send_bw.at[d], recv_bw.at[d], wide_peer(d))
         c.start()
         bias_first.append(c)
+    run[0] = jnp.zeros(run.shape[1:], run.dtype)
+    for fetch in loads:
+        fetch.wait()
+    unroll = 4
+
+    def backward(t, carry):
+        held = run[t * unroll]
+        for u in range(unroll):
+            k = t * unroll + u
+            held = held * table[2, k].astype(jnp.float32) + lax.dot_general(
+                adj[table[0, k]],
+                back[table[1, k]],
+                (((0,), (0,)), ((), ())),
+                preferred_element_type=jnp.float32,
+            )
+            run[k + 1] = held
+        return carry
+
+    early = (slots - row_blocks) // unroll
+    lax.fori_loop(0, early, backward, 0)
+    halo_blocks = ret.shape[0] * ret.shape[1] // side
+    per = ret.shape[1] // side
     for k in (2, 3, 1, 0):
         there, target = near[k]
+        for j in range(per):
+            ret[k, pl.ds(j * side, side), :] = run[table[3, k * per + j]].astype(ret.dtype)
 
         @pl.when(there)
         def _():
-            halo_copy(ret_ref, incoming, send, recv, k, target).start()
+            halo_copy(ret, incoming, send, recv, k, target).start()
 
         @pl.when(jnp.logical_not(there))
         def _():
@@ -353,6 +406,7 @@
         c.start()
         bias_first.append(c)
         second.append(c)
+    lax.fori_loop(early, slots // unroll, backward, 0)
     piece = part[n].astype(jnp.float32)
     for c in second:
         c.wait_recv()
@@ -368,6 +422,26 @@
         )
         c.start()
         third.append(c)
+    chunk = grad_ref.shape[1]
+    across = chunk // side
+    keep_to = nodes_live[0]
+
+    def own(i):
+        return jnp.concatenate(
+            [run[table[3, halo_blocks + i * across + j]] for j in range(across)], 0
+        )
+
+    def finish(i, full):
+        row = lax.broadcasted_iota(jnp.int32, full.shape, 0) + i * chunk
+        grad_ref[i] = jnp.where(row < keep_to, full, 0.0).astype(grad_ref.dtype)
+
+    low_chunks = row_blocks // across // 2
+
+    def high(i, carry):
+        finish(i, own(i))
+        return carry
+
+    lax.fori_loop(low_chunks, row_blocks // across, high, 0)
     for c in third:
         c.wait_recv()
     fourth = []
@@ -382,24 +456,19 @@
 
         @pl.when(there)
         def _():
-            halo_copy(ret_ref, incoming, send, recv, k, target).wait_send()
-            halo_copy(ret_ref, incoming, send, recv, k ^ 1, target).wait_recv()
-
-    fetch.wait()
-    chunk = low.shape[1]
-    merged = incoming[...].reshape(-1, incoming.shape[2])
+            halo_copy(ret, incoming, send, recv, k, target).wait_send()
+            halo_copy(ret, incoming, send, recv, k ^ 1, target).wait_recv()
+
+    merged = incoming[...].reshape(-1, width)
     idx = idx_ref[...]
-    keep_to = keep_ref[...]
 
     def scatter(i, carry):
         at = lax.broadcasted_iota(jnp.int32, (chunk, idx.shape[1]), 0) + i * chunk
         hot = jnp.where(at == idx, 1.0, 0.0).astype(jnp.bfloat16)
-        full = low[i] + jnp.dot(hot, merged, preferred_element_type=jnp.float32)
-        row = lax.broadcasted_iota(jnp.int32, full.shape, 0) + i * chunk
-        grad_ref[i] = jnp.where(row < keep_to, full, 0.0).astype(grad_ref.dtype)
-        return carry
-
-    lax.fori_loop(0, low.shape[0], scatter, 0)
+        finish(i, own(i) + jnp.dot(hot, merged, preferred_element_type=jnp.float32))
+        return carry
+
+    lax.fori_loop(0, low_chunks, scatter, 0)
     for c in fourth:
         c.wait_recv()
     for i in range(n_wide):
@@ -430,7 +499,6 @@
     row_blocks = nodes // side
     sides, halo = halo_index.shape[1:]
     halo_blocks = sides * halo // side
-    low_blocks = row_blocks // 2
     col_blocks = row_blocks + halo_blocks
     bf, f32 = jnp.bfloat16, jnp.float32
     picks = halo_index[0]
@@ -439,12 +507,17 @@
     hb = pl.BlockSpec(memory_space=ANY)
     dma = pltpu.SemaphoreType.DMA
 
-    halos = pl.pallas_call(
-        functools.partial(gather_kernel, n_wide, n_narrow),
+    lanes = -(-slots // 128) * 128
+    pad = ((0, 0), (0, lanes - slots))
+    halos, table = pl.pallas_call(
+        functools.partial(gather_kernel, n_wide, n_narrow, row_blocks, col_blocks),
         name="halo_out",
-        out_shape=jax.ShapeDtypeStruct((sides, halo, width), bf),
-        in_specs=[vm, hb],
-        out_specs=vm,
+        out_shape=(
+            jax.ShapeDtypeStruct((sides, halo, width), bf),
+            jax.ShapeDtypeStruct((8, lanes), jnp.int32),
+        ),
+        in_specs=[vm, vm, vm, vm, hb],
+        out_specs=(vm, vm),
         scratch_shapes=[
             pltpu.VMEM((nodes // 2, width), bf),
             pltpu.VMEM((sides, halo, width), bf),
@@ -455,28 +528,32 @@
         compiler_params=pltpu.CompilerParams(
             collective_id=0, has_side_effects=True, vmem_limit_bytes=VMEM_LIMIT
         ),
-    )(picks, features)
+    )(
+        picks,
+        jnp.pad(block_rows, pad),
+        jnp.pad(block_cols, pad),
+        jnp.broadcast_to(block_count[:, None], (1, lanes)),
+        features,
+    )
 
     step = 2
     blocked = (row_blocks, side, width)
-    out, low, high, ret, wg, bg = pl.pallas_call(
+    out, back, wg, bg = pl.pallas_call(
         functools.partial(layer_kernel, step),
         name="layer",
         out_shape=(
             jax.ShapeDtypeStruct(blocked, bf),
-            jax.ShapeDtypeStruct((low_blocks, side, width), f32),
-            jax.ShapeDtypeStruct((row_blocks - low_blocks, side, width), bf),
-            jax.ShapeDtypeStruct((halo_blocks, side, width), bf),
+            jax.ShapeDtypeStruct(blocked, bf),
             jax.ShapeDtypeStruct((width, width), bf),
             jax.ShapeDtypeStruct((1, width), f32),
         ),
         in_specs=[sm, sm, sm, sm, hb, hb, hb, hb, vm, vm],
-        out_specs=(hb, hb, hb, hb, vm, vm),
+        out_specs=(hb, hb, vm, vm),
         scratch_shapes=[
             pltpu.VMEM((col_blocks, side, width), bf),
             pltpu.VMEM((slots, side, side), bf),
             pltpu.VMEM(blocked, bf),
-            pltpu.VMEM((col_blocks + 1, side, width), f32),
+            pltpu.VMEM((row_blocks + 1, side, width), f32),
             pltpu.VMEM(blocked, bf),
             pltpu.VMEM(blocked, bf),
             pltpu.VMEM((width, width), f32),
@@ -502,18 +579,21 @@
     part_width = width // n_narrow
     scale = 1.0 / math.sqrt(nodes * n_wide * n_narrow)
     chunk = 2 * side
-    low_grad, wout, bout = pl.pallas_call(
-        functools.partial(sum_kernel, n_wide, n_narrow, scale),
-        name="sums",
+    input_grad, wout, bout = pl.pallas_call(
+        functools.partial(back_kernel, n_wide, n_narrow, scale),
+        name="back",
         out_shape=(
-            jax.ShapeDtypeStruct((low_blocks // 2, chunk, width), bf),
+            jax.ShapeDtypeStruct((nodes // chunk, chunk, width), bf),
             jax.ShapeDtypeStruct((width, width), f32),
             jax.ShapeDtypeStruct((1, width), f32),
         ),
-        in_specs=[vm, vm, vm, vm, vm, hb],
+        in_specs=[sm, sm, vm, vm, vm, hb, hb],
         out_specs=(vm, vm, vm),
         scratch_shapes=[
-            pltpu.VMEM((low_blocks // 2, chunk, width), f32),
+            pltpu.VMEM((slots, side, side), bf),
+            pltpu.VMEM(blocked, bf),
+            pltpu.VMEM((slots + 1, side, width), f32),
+            pltpu.VMEM((sides, halo, width), bf),
             pltpu.VMEM((sides, halo, width), bf),
             pltpu.VMEM((n_wide, slab, width), bf),
             pltpu.VMEM((n_narrow, slab, part_width), bf),
@@ -523,7 +603,7 @@
             pltpu.VMEM((n_wide, 1, width), f32),
             pltpu.VMEM((1, width), f32),
             pltpu.VMEM((n_narrow, 1, width), f32),
-            dma,
+            dma((2,)),
             dma((sides,)),
             dma((sides,)),
         ]
@@ -535,17 +615,15 @@
             collective_id=1, has_side_effects=True, vmem_limit_bytes=VMEM_LIMIT
         ),
     )(
+        table,
+        node_count,
         picks.reshape(1, sides * halo),
-        jnp.broadcast_to(node_count.reshape(1, 1), (1, width)),
-        ret.reshape(sides, halo, width),
         wg.reshape(n_wide, slab, width),
         bg,
-        low.reshape(low_blocks // 2, chunk, width),
+        adjacency,
+        back,
     )
-    input_grad = jnp.concatenate(
-        [low_grad.reshape(-1, width), high.reshape(-1, width)], 0
-    )
-    return out.reshape(nodes, width), input_grad, wout, bout.reshape(width)
+    return out.reshape(nodes, width), input_grad.reshape(nodes, width), wout, bout.reshape(width)
 
 
 def solution(mesh):

time: 90.6 us -> 87.6 us (0.967)
  local copies, waits for them, and re-layouts: 3.43 us -> 10.2 us
  Pallas kernels: 81.4 us -> 74.7 us
  other arithmetic: 3.96 us -> 0 us
    pallas_call x1, Pallas kernels: 36.2 us -> 28.2 us  [local(): pl.pallas_call(functools.partial(layer_kernel, step), name='layer', out_s...]
    unnamed x9 -> x8, local copies, waits for them, and re-layouts: 2.84 us -> 7.4 us
    concatenate x1 -> x0, other arithmetic: 3.96 us -> none  [local(): jnp.concatenate([low_grad.reshape(-1, width), high.reshape(-1, width)], 0)]
    pad x0 -> x2, local copies, waits for them, and re-layouts: none -> 2.34 us  [the longest x1 1.17 us: local(): jnp.pad(block_rows, pad)]
    pallas_call x2, Pallas kernels: 45.1 us -> 46.5 us  [the longest x1 33.1 us: local(): pl.pallas_call(functools.partial(back_kernel, n_wide, n_narrow, scale), n...]
where the time goes in v2:
time: 87.6 us; the launch traced here: 86.9 us
  Pallas kernels  74.7 us (85%)
  local copies, waits for them, and re-layouts  10.2 us (12%)
  between operations  1.97 us (2%)
    pallas_call x1, Pallas kernels, local(): pl.pallas_call(functools.partial(back_kernel, n_wide, n_narrow, scale), n...  33.1 us
    pallas_call x1, Pallas kernels, local(): pl.pallas_call(functools.partial(layer_kernel, step), name='layer', out_s...  28.2 us
    pallas_call x1, Pallas kernels, local(): pl.pallas_call(functools.partial(gather_kernel, n_wide, n_narrow, row_blo...  13.4 us
    unnamed x8, local copies, waits for them, and re-layouts  7.4 us

profile of v2, /device:TPU:0, one launch (start us, length us, event | category | flops | bytes accessed | tf_op | source)
XLA Modules:
  0.0 86.9 jit_solution(11186428574454211023)
XLA Ops:
  1.9 1.2 %pad.7.row_ref = s32[1,128]{1,0:T(1,128)} pad(s32[1,96]{1,0:T(1,128)} %param.12, s32[]{:T(128)} %constant.0.clone.1), padding=0_0x0_32 | pad | bytes 900 | tf_op jit(solution)/shard_map/jit(_pad)/pad | solution.py:533
  3.1 1.2 %pad.8.col_ref = s32[1,128]{1,0:T(1,128)} pad(s32[1,96]{1,0:T(1,128)} %param.13, s32[]{:T(128)} %constant.0.clone.1), padding=0_0x0_32 | pad | bytes 900 | tf_op jit(solution)/shard_map/jit(_pad)/pad | solution.py:534
  4.3 0.5 broadcast_in_dim.9.count_ref
  4.8 1.3 %copy.14 = s32[1,1,4,256]{3,1,2,0:T(1,128)} copy(s32[1,1,4,256]{3,2,1,0:T(4,128)} %bitcast.21) | data formatting | bytes 8192
  6.1 13.4 %halo_out.1 = (bf16[4,256,512]{2,1,0:T(8,128)(2,1)}, s32[8,128]{1,0:T(8,128)}) custom-call(s32[4,256]{1,0:T(4,128)} %bitcast.22, s32[1,128]{1,0:T(1,128)} %pad.7.row_ref, s32[1,128]{1,0:T(1,128)} %pad.8.col_ref, s32[1,128]{1,0:T(1,128)} %broadcast_in_dim.9.count_ref, bf16[4096,512]{1,0:T(8,128)(2,1)} %feat_hbm.1), custom_call_target="tpu_custom_call" | custom-call | tf_op jit(solution)/shard_map/halo_out/pallas_call | solution.py:512
  19.5 28.2 %layer.1 = (bf16[32,128,512]{2,1,0:T(8,128)(2,1)}, bf16[32,128,512]{2,1,0:T(8,128)(2,1)}, bf16[512,512]{1,0:T(8,128)(2,1)}, f32[1,512]{1,0:T(1,128)}) custom-call(s32[96]{0:T(128)} %bitcast.25, s32[96]{0:T(128)} %bitcast.26, s32[1]{0:T(128)} %copy.18.live, s32[1]{0:T(128)S(6)} %copy.19.nodes_live, bf16[32,128,512]{2,1,0:T(8,128)(2,1)} %bitcast.15, ...), custom_call_target="tpu_custom_call" | custom-call | tf_op jit(solution)/shard_map/layer/pallas_call | solution.py:541
  47.7 33.1 %back.1 = (bf16[16,256,512]{2,1,0:T(8,128)(2,1)}, f32[512,512]{1,0:T(8,128)}, f32[1,512]{1,0:T(1,128)}) custom-call(s32[8,128]{1,0:T(8,128)} %get-tuple-element.15.table, s32[1]{0:T(128)S(6)} %copy.19.nodes_live, s32[1,1024]{1,0:T(1,128)} %bitcast.20, bf16[8,64,512]{2,1,0:T(8,128)(2,1)} %bitcast.19, f32[1,512]{1,0:T(1,128)} %get-tuple-element.17.bg_ref, ...), custom_call_target="tpu_custom_call" | custom-call | tf_op jit(solution)/shard_map/back/pallas_call | solution.py:582
  80.8 0.0 copy-start
  80.8 0.0 copy-start.1
  80.8 4.6 %copy.20 = bf16[4096,512]{1,0:T(8,128)(2,1)} copy(bf16[4096,512]{1,0:T(8,128)(2,1)} %bitcast.17) | data formatting | bytes 8388608
  85.3 0.0 copy-done
  85.3 1.0 %copy.21 = f32[512,512]{1,0:T(8,128)} copy(f32[512,512]{1,0:T(8,128)S(1)} %copy-done) | data formatting | bytes 2097152
  86.3 0.0 copy-done.1
  86.3 0.6 copy.22
Async XLA Ops:
  80.8 4.6 %copy-start = (f32[512,512]{1,0:T(8,128)S(1)}, f32[512,512]{1,0:T(8,128)}, u32[]{:S(2)}) copy-start(f32[512,512]{1,0:T(8,128)} %get-tuple-element.28) | copy-start | bytes 3145732
  80.8 5.5 %copy-start.1 = (f32[1,512]{1,0:T(1,128)S(1)}, f32[1,512]{1,0:T(1,128)}, u32[]{:S(2)}) copy-start(f32[1,512]{1,0:T(1,128)} %get-tuple-element.21) | copy-start | bytes 6148

commit v3 on v2

--- a/solution.py
+++ b/solution.py
@@ -35,9 +35,13 @@
     )
 
 
-def tables(row_ref, col_ref, count, row_blocks, col_blocks):
-    lanes = row_ref.shape[1]
+def tables(row_ref, col_ref, pads, count, row_blocks, col_blocks):
+    lanes = pads.shape[1]
+    slots = row_ref.shape[1]
     f32 = jnp.float32
+    pads[...] = jnp.zeros_like(pads)
+    pads[0:1, 0:slots] = row_ref[...]
+    pads[1:2, 0:slots] = col_ref[...]
     lane = lax.broadcasted_iota(jnp.int32, (lanes, lanes), 1).astype(f32)
     sub = lax.broadcasted_iota(jnp.int32, (lanes, lanes), 0).astype(f32)
 
@@ -45,11 +49,11 @@
         return jnp.broadcast_to(x.astype(f32), (lanes, lanes))
 
     halo_blocks = col_blocks - row_blocks
-    col = spread(col_ref[...])
+    col = spread(pads[1:2, :])
     place = jnp.where(col >= row_blocks, col - row_blocks, col + halo_blocks)
-    place = jnp.where(lane < spread(count), place, float(col_blocks))
+    place = jnp.where(lane < count.astype(f32), place, float(col_blocks))
     place_t = jnp.transpose(place)
-    row_t = jnp.transpose(spread(row_ref[...]))
+    row_t = jnp.transpose(spread(pads[0:1, :]))
     same = place == place_t
     ahead = lane < sub
     one = lambda m: jnp.where(m, 1.0, 0.0)
@@ -74,13 +78,14 @@
     feat_hbm,
     halo_ref,
     table_ref,
+    pads,
     feat,
     packed,
     load,
     send,
     recv,
 ):
-    count = idx_ref.shape[1]
+    count = idx_ref.shape[2]
     span = feat.shape[0]
     fetch = pltpu.make_async_copy(feat_hbm.at[pl.ds(0, span)], feat, load)
     fetch.start()
@@ -96,7 +101,7 @@
     lane = lax.broadcasted_iota(jnp.int32, (count, 128), 1).astype(jnp.float32)
 
     def pack(k):
-        row = idx_ref[pl.ds(k, 1), :].astype(jnp.float32)
+        row = idx_ref[0, pl.ds(k, 1), :].astype(jnp.float32)
         column = jnp.transpose(jnp.broadcast_to(row, (128, count)))
         hot = jnp.concatenate(
             [
@@ -126,7 +131,7 @@
 
     table_ref[...] = jnp.zeros_like(table_ref)
     for i, line in enumerate(
-        tables(row_ref, col_ref, count_ref[...], row_blocks, col_blocks)
+        tables(row_ref, col_ref, pads, count_ref[0], row_blocks, col_blocks)
     ):
         table_ref[pl.ds(i, 1), :] = line.astype(jnp.int32)
 
@@ -219,10 +224,14 @@
 
     tall = step * side
 
-    def dense(i, carry):
+    def into(i):
         at = pl.ds(i * step, step)
         agg = acc[at].reshape(tall, width).astype(jnp.bfloat16)
-        pre = jnp.dot(agg, w_ref[...], preferred_element_type=jnp.float32) + b_ref[...]
+        return agg, jnp.dot(agg, w_ref[...], preferred_element_type=jnp.float32)
+
+    def middle(i, pre):
+        at = pl.ds(i * step, step)
+        pre = pre + b_ref[...]
         keep = kept(i * step, step)
         sig = 0.5 * jnp.tanh(0.5 * pre) + 0.5
         act = pre * sig
@@ -230,20 +239,34 @@
         put(i).start()
         g = grad[at].reshape(tall, width).astype(jnp.float32)
         dpre = jnp.where(keep, g * (sig + act * (1.0 - sig)), 0.0).astype(jnp.bfloat16)
+        bsum[...] += jnp.sum(dpre.astype(jnp.float32).reshape(tall // 8, 8, width), 0)
+        return dpre
+
+    def after(i, agg, dpre):
         wsum[...] += lax.dot_general(
             agg, dpre, (((0,), (0,)), ((), ())), preferred_element_type=jnp.float32
         )
-        bsum[...] += jnp.sum(dpre.astype(jnp.float32).reshape(tall // 8, 8, width), 0)
-        back[at] = (
+        back[pl.ds(i * step, step)] = (
             lax.dot_general(
                 dpre, w_ref[...], (((1,), (1,)), ((), ())), preferred_element_type=jnp.float32
             )
             .astype(jnp.bfloat16)
             .reshape(step, side, width)
         )
-        return carry
-
-    lax.fori_loop(0, row_blocks // step, dense, 0)
+
+    group = 4
+
+    def dense(t, carry):
+        now = into(t * group)
+        for u in range(group):
+            i = t * group + u
+            later = into(i + 1) if u + 1 < group else None
+            dpre = middle(i, now[1])
+            after(i, now[0], dpre)
+            now = later
+        return carry
+
+    lax.fori_loop(0, row_blocks // step // group, dense, 0)
     wg_ref[...] = wsum[...].astype(wg_ref.dtype)
     bg_ref[...] = jnp.sum(bsum[...], 0, keepdims=True)
 
@@ -269,9 +292,11 @@
     bg_ref,
     adj_hbm,
     back_hbm,
-    grad_ref,
+    grad_hbm,
     wout_ref,
     bout_ref,
+    grad_ref,
+    grad_sem,
     adj,
     back,
     run,
@@ -431,9 +456,13 @@
             [run[table[3, halo_blocks + i * across + j]] for j in range(across)], 0
         )
 
+    def leave(i):
+        return pltpu.make_async_copy(grad_ref.at[i], grad_hbm.at[i], grad_sem.at[i])
+
     def finish(i, full):
         row = lax.broadcasted_iota(jnp.int32, full.shape, 0) + i * chunk
         grad_ref[i] = jnp.where(row < keep_to, full, 0.0).astype(grad_ref.dtype)
+        leave(i).start()
 
     low_chunks = row_blocks // across // 2
 
@@ -460,7 +489,7 @@
             halo_copy(ret, incoming, send, recv, k ^ 1, target).wait_recv()
 
     merged = incoming[...].reshape(-1, width)
-    idx = idx_ref[...]
+    idx = jnp.concatenate([idx_ref[0, k : k + 1, :] for k in range(4)], 1)
 
     def scatter(i, carry):
         at = lax.broadcasted_iota(jnp.int32, (chunk, idx.shape[1]), 0) + i * chunk
@@ -476,8 +505,28 @@
             wout_ref[pl.ds(i * slab, slab), pl.ds(j * part_width, part_width)] = ag_wide[
                 i, j
             ].astype(jnp.float32)
+    def drain(i, carry):
+        leave(i).wait()
+        return carry
+
+    lax.fori_loop(0, row_blocks // across, drain, 0)
     for c in first + bias_first + second[: n_narrow - 1] + third + fourth:
         c.wait_send()
+
+
+def hand_on(grad_in, w_in, b_in, grad_out, w_out, b_out, grad, wg, bg, take, give):
+    pieces = grad.shape[0]
+    hops = [(grad_in.at[i], grad.at[i], grad_out.at[i]) for i in range(pieces)]
+    hops += [(w_in, wg, w_out), (b_in, bg, b_out)]
+    ins = [pltpu.make_async_copy(a, b, take.at[i]) for i, (a, b, _) in enumerate(hops)]
+    outs = [pltpu.make_async_copy(b, c, give.at[i]) for i, (_, b, c) in enumerate(hops)]
+    for c in ins:
+        c.start()
+    for c, d in zip(ins, outs):
+        c.wait()
+        d.start()
+    for d in outs:
+        d.wait()
 
 
 def local(
@@ -501,14 +550,12 @@
     halo_blocks = sides * halo // side
     col_blocks = row_blocks + halo_blocks
     bf, f32 = jnp.bfloat16, jnp.float32
-    picks = halo_index[0]
     vm = pl.BlockSpec(memory_space=pltpu.VMEM)
     sm = pl.BlockSpec(memory_space=pltpu.SMEM)
     hb = pl.BlockSpec(memory_space=ANY)
     dma = pltpu.SemaphoreType.DMA
 
     lanes = -(-slots // 128) * 128
-    pad = ((0, 0), (0, lanes - slots))
     halos, table = pl.pallas_call(
         functools.partial(gather_kernel, n_wide, n_narrow, row_blocks, col_blocks),
         name="halo_out",
@@ -516,9 +563,10 @@
             jax.ShapeDtypeStruct((sides, halo, width), bf),
             jax.ShapeDtypeStruct((8, lanes), jnp.int32),
         ),
-        in_specs=[vm, vm, vm, vm, hb],
+        in_specs=[vm, vm, vm, sm, hb],
         out_specs=(vm, vm),
         scratch_shapes=[
+            pltpu.VMEM((8, lanes), jnp.int32),
             pltpu.VMEM((nodes // 2, width), bf),
             pltpu.VMEM((sides, halo, width), bf),
             dma,
@@ -529,10 +577,10 @@
             collective_id=0, has_side_effects=True, vmem_limit_bytes=VMEM_LIMIT
         ),
     )(
-        picks,
-        jnp.pad(block_rows, pad),
-        jnp.pad(block_cols, pad),
-        jnp.broadcast_to(block_count[:, None], (1, lanes)),
+        halo_index,
+        block_rows,
+        block_cols,
+        block_count,
         features,
     )
 
@@ -588,8 +636,10 @@
             jax.ShapeDtypeStruct((1, width), f32),
         ),
         in_specs=[sm, sm, vm, vm, vm, hb, hb],
-        out_specs=(vm, vm, vm),
+        out_specs=(hb, vm, vm),
         scratch_shapes=[
+            pltpu.VMEM((nodes // chunk, chunk, width), bf),
+            dma((nodes // chunk,)),
             pltpu.VMEM((slots, side, side), bf),
             pltpu.VMEM(blocked, bf),
             pltpu.VMEM((slots + 1, side, width), f32),
@@ -617,12 +667,32 @@
     )(
         table,
         node_count,
-        picks.reshape(1, sides * halo),
+        halo_index,
         wg.reshape(n_wide, slab, width),
         bg,
         adjacency,
         back,
     )
+    pieces = 8
+    input_grad, wout, bout = pl.pallas_call(
+        hand_on,
+        name="hand_on",
+        out_shape=(
+            jax.ShapeDtypeStruct((pieces, nodes // pieces, width), bf),
+            jax.ShapeDtypeStruct((width, width), f32),
+            jax.ShapeDtypeStruct((1, width), f32),
+        ),
+        in_specs=[hb, hb, hb],
+        out_specs=(hb, hb, hb),
+        scratch_shapes=[
+            pltpu.VMEM((pieces, nodes // pieces, width), bf),
+            pltpu.VMEM((width, width), f32),
+            pltpu.VMEM((1, width), f32),
+            dma((pieces + 2,)),
+            dma((pieces + 2,)),
+        ],
+        compiler_params=pltpu.CompilerParams(vmem_limit_bytes=VMEM_LIMIT),
+    )(input_grad.reshape(pieces, nodes // pieces, width), wout, bout)
     return out.reshape(nodes, width), input_grad.reshape(nodes, width), wout, bout.reshape(width)
 
 

time: 87.6 us -> 78.2 us (0.89)
  local copies, waits for them, and re-layouts: 10.2 us -> 0 us
  Pallas kernels: 74.7 us -> 75.9 us
    unnamed x8 -> x0, local copies, waits for them, and re-layouts: 7.4 us -> none
    pallas_call x0 -> x1, Pallas kernels: none -> 4.92 us  [local(): pl.pallas_call(hand_on, name='hand_on', out_shape=(jax.ShapeDtypeStruct((...]
    pallas_call x1, Pallas kernels: 28.2 us -> 23.9 us  [local(): pl.pallas_call(functools.partial(layer_kernel, step), name='layer', out_s...]
    pad x2 -> x0, local copies, waits for them, and re-layouts: 2.34 us -> none  [the longest x1 1.17 us: local(): jnp.pad(block_rows, pad)]
where the time goes in v3:
time: 78.2 us; the launch traced here: 77.9 us
  Pallas kernels  75.9 us (97%)
  between operations  1.95 us (2%)
    pallas_call x1, Pallas kernels, local(): pl.pallas_call(functools.partial(back_kernel, n_wide, n_narrow, scale), n...  33.7 us
    pallas_call x1, Pallas kernels, local(): pl.pallas_call(functools.partial(layer_kernel, step), name='layer', out_s...  23.9 us
    pallas_call x1, Pallas kernels, local(): pl.pallas_call(functools.partial(gather_kernel, n_wide, n_narrow, row_blo...  13.5 us
    pallas_call x1, Pallas kernels, local(): pl.pallas_call(hand_on, name='hand_on', out_shape=(jax.ShapeDtypeStruct((...  4.92 us

profile of v3, /device:TPU:0, one launch (start us, length us, event | category | flops | bytes accessed | tf_op | source)
XLA Modules:
  0.0 77.9 jit_solution(13012645356038745875)
XLA Ops:
  1.9 13.5 %halo_out.1 = (bf16[4,256,512]{2,1,0:T(8,128)(2,1)}, s32[8,128]{1,0:T(8,128)}) custom-call(s32[1,4,256]{2,1,0:T(4,128)} %idx_ref.3, s32[1,96]{1,0:T(1,128)} %row_ref.1, s32[1,96]{1,0:T(1,128)} %col_ref.1, s32[1]{0:T(128)S(6)} %copy.14.count_ref.live, bf16[4096,512]{1,0:T(8,128)(2,1)} %feat_hbm.1), custom_call_target="tpu_custom_call" | custom-call | tf_op jit(solution)/shard_map/halo_out/pallas_call | solution.py:559
  15.4 23.9 %layer.1 = (bf16[32,128,512]{2,1,0:T(8,128)(2,1)}, bf16[32,128,512]{2,1,0:T(8,128)(2,1)}, bf16[512,512]{1,0:T(8,128)(2,1)}, f32[1,512]{1,0:T(1,128)}) custom-call(s32[96]{0:T(128)} %bitcast.17, s32[96]{0:T(128)} %bitcast.18, s32[1]{0:T(128)S(6)} %copy.14.count_ref.live, s32[1]{0:T(128)S(6)} %copy.15.nodes_live, bf16[32,128,512]{2,1,0:T(8,128)(2,1)} %bitcast.11, ...), custom_call_target="tpu_custom_call" | custom-call | tf_op jit(solution)/shard_map/layer/pallas_call | solution.py:589
  39.3 33.7 %back.1 = (bf16[16,256,512]{2,1,0:T(8,128)(2,1)}, f32[512,512]{1,0:T(8,128)}, f32[1,512]{1,0:T(1,128)}) custom-call(s32[8,128]{1,0:T(8,128)} %get-tuple-element.18.table, s32[1]{0:T(128)S(6)} %copy.15.nodes_live, s32[1,4,256]{2,1,0:T(4,128)} %idx_ref.3, bf16[8,64,512]{2,1,0:T(8,128)(2,1)} %bitcast.15, f32[1,512]{1,0:T(1,128)} %get-tuple-element.20.bg_ref, ...), custom_call_target="tpu_custom_call" | custom-call | tf_op jit(solution)/shard_map/back/pallas_call | solution.py:630
  73.0 4.9 %hand_on.1 = (bf16[8,512,512]{2,1,0:T(8,128)(2,1)}, f32[512,512]{1,0:T(8,128)}, f32[1,512]{1,0:T(1,128)}) custom-call(bf16[8,512,512]{2,1,0:T(8,128)(2,1)} %bitcast.12, f32[512,512]{1,0:T(8,128)} %get-tuple-element.23.w_in, f32[1,512]{1,0:T(1,128)} %get-tuple-element.24.b_in), custom_call_target="tpu_custom_call" | custom-call | tf_op jit(solution)/shard_map/hand_on/pallas_call | solution.py:677

commit v4 on v3

--- a/solution.py
+++ b/solution.py
@@ -170,6 +170,7 @@
     bsum,
     sem,
     out_sem,
+    back_sem,
 ):
     row_blocks, side, width = feat_hbm.shape
     halo_blocks = halo_hbm.shape[0]
@@ -181,7 +182,7 @@
         pltpu.make_async_copy(adj_hbm, adj, sem.at[2]),
         pltpu.make_async_copy(grad_hbm, grad, sem.at[3]),
     ]
-    for load in loads:
+    for load in loads[:3]:
         load.start()
 
     def clear(i, carry):
@@ -193,6 +194,7 @@
     bsum[...] = jnp.zeros_like(bsum)
     for load in loads[:3]:
         load.wait()
+    loads[3].start()
 
     def kept(block, blocks=1):
         at = lax.broadcasted_iota(jnp.int32, (blocks * side, width), 0)
@@ -204,7 +206,7 @@
 
     lax.fori_loop(keep_to // side, row_blocks, mask, 0)
 
-    unroll = 4
+    unroll = 8
     trips = (count + unroll - 1) // unroll
 
     def forward(t, carry):
@@ -220,6 +222,11 @@
     def put(i):
         return pltpu.make_async_copy(
             out.at[pl.ds(i * step, step)], out_hbm.at[pl.ds(i * step, step)], out_sem.at[i]
+        )
+
+    def put_back(i):
+        return pltpu.make_async_copy(
+            back.at[pl.ds(i * step, step)], back_hbm.at[pl.ds(i * step, step)], back_sem.at[i]
         )
 
     tall = step * side
@@ -253,6 +260,7 @@
             .astype(jnp.bfloat16)
             .reshape(step, side, width)
         )
+        put_back(i).start()
 
     group = 4
 
@@ -270,12 +278,9 @@
     wg_ref[...] = wsum[...].astype(wg_ref.dtype)
     bg_ref[...] = jnp.sum(bsum[...], 0, keepdims=True)
 
-    kept_back = pltpu.make_async_copy(back, back_hbm, sem.at[0])
-    kept_back.start()
-    kept_back.wait()
-
     def drain(i, carry):
         put(i).wait()
+        put_back(i).wait()
         return carry
 
     lax.fori_loop(0, row_blocks // step, drain, 0)
@@ -375,7 +380,7 @@
     run[0] = jnp.zeros(run.shape[1:], run.dtype)
     for fetch in loads:
         fetch.wait()
-    unroll = 4
+    unroll = 8
 
     def backward(t, carry):
         held = run[t * unroll]
@@ -607,6 +612,7 @@
             pltpu.VMEM((width, width), f32),
             pltpu.VMEM((8, width), f32),
             dma((4,)),
+            dma((row_blocks // step,)),
             dma((row_blocks // step,)),
         ],
         compiler_params=pltpu.CompilerParams(vmem_limit_bytes=VMEM_LIMIT),

time: 78.2 us -> 74.7 us (0.955)
  Pallas kernels: 75.9 us -> 72.3 us
    pallas_call x1, Pallas kernels: 33.7 us -> 31.7 us  [local(): pl.pallas_call(functools.partial(back_kernel, n_wide, n_narrow, scale), n...]
    pallas_call x1, Pallas kernels: 23.9 us -> 22.2 us  [local(): pl.pallas_call(functools.partial(layer_kernel, step), name='layer', out_s...]
where the time goes in v4:
time: 74.7 us; the launch traced here: 74.3 us
  Pallas kernels  72.3 us (97%)
  between operations  1.95 us (3%)
    pallas_call x1, Pallas kernels, local(): pl.pallas_call(functools.partial(back_kernel, n_wide, n_narrow, scale), n...  31.7 us
    pallas_call x1, Pallas kernels, local(): pl.pallas_call(functools.partial(layer_kernel, step), name='layer', out_s...  22.2 us
    pallas_call x1, Pallas kernels, local(): pl.pallas_call(functools.partial(gather_kernel, n_wide, n_narrow, row_blo...  13.5 us
    pallas_call x1, Pallas kernels, local(): pl.pallas_call(hand_on, name='hand_on', out_shape=(jax.ShapeDtypeStruct((...  4.92 us

profile of v4, /device:TPU:0, one launch (start us, length us, event | category | flops | bytes accessed | tf_op | source)
XLA Modules:
  0.0 74.3 jit_solution(12990095800805686152)
XLA Ops:
  1.9 13.5 %halo_out.1 = (bf16[4,256,512]{2,1,0:T(8,128)(2,1)}, s32[8,128]{1,0:T(8,128)}) custom-call(s32[1,4,256]{2,1,0:T(4,128)} %idx_ref.3, s32[1,96]{1,0:T(1,128)} %row_ref.1, s32[1,96]{1,0:T(1,128)} %col_ref.1, s32[1]{0:T(128)S(6)} %copy.14.count_ref.live, bf16[4096,512]{1,0:T(8,128)(2,1)} %feat_hbm.1), custom_call_target="tpu_custom_call" | custom-call | tf_op jit(solution)/shard_map/halo_out/pallas_call | solution.py:564
  15.4 22.2 %layer.1 = (bf16[32,128,512]{2,1,0:T(8,128)(2,1)}, bf16[32,128,512]{2,1,0:T(8,128)(2,1)}, bf16[512,512]{1,0:T(8,128)(2,1)}, f32[1,512]{1,0:T(1,128)}) custom-call(s32[96]{0:T(128)} %bitcast.17, s32[96]{0:T(128)} %bitcast.18, s32[1]{0:T(128)S(6)} %copy.14.count_ref.live, s32[1]{0:T(128)S(6)} %copy.15.nodes_live, bf16[32,128,512]{2,1,0:T(8,128)(2,1)} %bitcast.11, ...), custom_call_target="tpu_custom_call" | custom-call | tf_op jit(solution)/shard_map/layer/pallas_call | solution.py:594
  37.6 31.7 %back.1 = (bf16[16,256,512]{2,1,0:T(8,128)(2,1)}, f32[512,512]{1,0:T(8,128)}, f32[1,512]{1,0:T(1,128)}) custom-call(s32[8,128]{1,0:T(8,128)} %get-tuple-element.18.table, s32[1]{0:T(128)S(6)} %copy.15.nodes_live, s32[1,4,256]{2,1,0:T(4,128)} %idx_ref.3, bf16[8,64,512]{2,1,0:T(8,128)(2,1)} %bitcast.15, f32[1,512]{1,0:T(1,128)} %get-tuple-element.20.bg_ref, ...), custom_call_target="tpu_custom_call" | custom-call | tf_op jit(solution)/shard_map/back/pallas_call | solution.py:636
  69.4 4.9 %hand_on.1 = (bf16[8,512,512]{2,1,0:T(8,128)(2,1)}, f32[512,512]{1,0:T(8,128)}, f32[1,512]{1,0:T(1,128)}) custom-call(bf16[8,512,512]{2,1,0:T(8,128)(2,1)} %bitcast.12, f32[512,512]{1,0:T(8,128)} %get-tuple-element.23.w_in, f32[1,512]{1,0:T(1,128)} %get-tuple-element.24.b_in), custom_call_target="tpu_custom_call" | custom-call | tf_op jit(solution)/shard_map/hand_on/pallas_call | solution.py:683

commit v5 on v4

--- a/solution.py
+++ b/solution.py
@@ -206,7 +206,7 @@
 
     lax.fori_loop(keep_to // side, row_blocks, mask, 0)
 
-    unroll = 8
+    unroll = 16
     trips = (count + unroll - 1) // unroll
 
     def forward(t, carry):
@@ -262,7 +262,7 @@
         )
         put_back(i).start()
 
-    group = 4
+    group = 8
 
     def dense(t, carry):
         now = into(t * group)
@@ -380,7 +380,7 @@
     run[0] = jnp.zeros(run.shape[1:], run.dtype)
     for fetch in loads:
         fetch.wait()
-    unroll = 8
+    unroll = 16
 
     def backward(t, carry):
         held = run[t * unroll]

time: 74.7 us -> 73.7 us (0.987)
  Pallas kernels: 72.3 us -> 71.1 us
    pallas_call x1, Pallas kernels: 31.7 us -> 29.9 us  [local(): pl.pallas_call(functools.partial(back_kernel, n_wide, n_narrow, scale), n...]
where the time goes in v5:
time: 73.7 us; the launch traced here: 73.1 us
  Pallas kernels  71.1 us (96%)
  between operations  1.95 us (3%)
    pallas_call x1, Pallas kernels, local(): pl.pallas_call(functools.partial(back_kernel, n_wide, n_narrow, scale), n...  29.9 us
    pallas_call x1, Pallas kernels, local(): pl.pallas_call(functools.partial(layer_kernel, step), name='layer', out_s...  22.8 us
    pallas_call x1, Pallas kernels, local(): pl.pallas_call(functools.partial(gather_kernel, n_wide, n_narrow, row_blo...  13.5 us
    pallas_call x1, Pallas kernels, local(): pl.pallas_call(hand_on, name='hand_on', out_shape=(jax.ShapeDtypeStruct((...  4.92 us

profile of v5, /device:TPU:0, one launch (start us, length us, event | category | flops | bytes accessed | tf_op | source)
XLA Modules:
  0.0 73.1 jit_solution(18181831227024638913)
XLA Ops:
  1.9 13.5 %halo_out.1 = (bf16[4,256,512]{2,1,0:T(8,128)(2,1)}, s32[8,128]{1,0:T(8,128)}) custom-call(s32[1,4,256]{2,1,0:T(4,128)} %idx_ref.3, s32[1,96]{1,0:T(1,128)} %row_ref.1, s32[1,96]{1,0:T(1,128)} %col_ref.1, s32[1]{0:T(128)S(6)} %copy.14.count_ref.live, bf16[4096,512]{1,0:T(8,128)(2,1)} %feat_hbm.1), custom_call_target="tpu_custom_call" | custom-call | tf_op jit(solution)/shard_map/halo_out/pallas_call | solution.py:564
  15.4 22.8 %layer.1 = (bf16[32,128,512]{2,1,0:T(8,128)(2,1)}, bf16[32,128,512]{2,1,0:T(8,128)(2,1)}, bf16[512,512]{1,0:T(8,128)(2,1)}, f32[1,512]{1,0:T(1,128)}) custom-call(s32[96]{0:T(128)} %bitcast.17, s32[96]{0:T(128)} %bitcast.18, s32[1]{0:T(128)S(6)} %copy.14.count_ref.live, s32[1]{0:T(128)S(6)} %copy.15.nodes_live, bf16[32,128,512]{2,1,0:T(8,128)(2,1)} %bitcast.11, ...), custom_call_target="tpu_custom_call" | custom-call | tf_op jit(solution)/shard_map/layer/pallas_call | solution.py:594
  38.2 29.9 %back.1 = (bf16[16,256,512]{2,1,0:T(8,128)(2,1)}, f32[512,512]{1,0:T(8,128)}, f32[1,512]{1,0:T(1,128)}) custom-call(s32[8,128]{1,0:T(8,128)} %get-tuple-element.18.table, s32[1]{0:T(128)S(6)} %copy.15.nodes_live, s32[1,4,256]{2,1,0:T(4,128)} %idx_ref.3, bf16[8,64,512]{2,1,0:T(8,128)(2,1)} %bitcast.15, f32[1,512]{1,0:T(1,128)} %get-tuple-element.20.bg_ref, ...), custom_call_target="tpu_custom_call" | custom-call | tf_op jit(solution)/shard_map/back/pallas_call | solution.py:636
  68.1 4.9 %hand_on.1 = (bf16[8,512,512]{2,1,0:T(8,128)(2,1)}, f32[512,512]{1,0:T(8,128)}, f32[1,512]{1,0:T(1,128)}) custom-call(bf16[8,512,512]{2,1,0:T(8,128)(2,1)} %bitcast.12, f32[512,512]{1,0:T(8,128)} %get-tuple-element.23.w_in, f32[1,512]{1,0:T(1,128)} %get-tuple-element.24.b_in), custom_call_target="tpu_custom_call" | custom-call | tf_op jit(solution)/shard_map/hand_on/pallas_call | solution.py:683
